TPU v7x, 32 devices: a whole 2x2x4 slice. The times are simulated.
32 devices in a mesh: dp: 8 (over z, x), tm: 4 (over y, core).
Axes of the slice: x: 2, y: 2, z: 4, core: 2. Of those that a mesh axis runs over, the one named last changes fastest.
Arguments:
- frames: bfloat16 [8, 512, 1536], P('dp', 'tm'), may hold values from -3 to 3
- query: bfloat16 [8, 512, 1536], P('dp', 'tm'), may hold values from -6 to 6
- keys: bfloat16 [8, 512, 1536], P('dp', 'tm'), may hold values from -6 to 6
- values: bfloat16 [8, 512, 1536], P('dp', 'tm'), may hold values from -6 to 6
- norm_gain: float32 [1536], replicated, may hold values from 0.1 to 1.9
- conv_gain: float32 [1536], replicated, may hold values from 0.1 to 1.9
- w_glu: bfloat16 [1536, 3072], P('tm'), may hold values from -0.15625 to 0.15625
- taps: float32 [32, 1536], replicated, may hold values from -1 to 1
- w_out: bfloat16 [1536, 1536], P('tm'), may hold values from -0.15625 to 0.15625
- cotangent: bfloat16 [8, 512, 1536], P('dp', 'tm'), may hold values from -0.09375 to 0.09375
Outputs:
- glu_grad: float32 [1536, 3072], P('tm')
- taps_grad: float32 [32, 1536], P(None, 'tm')
- out_grad: float32 [1536, 1536], P('tm')
All inputs are finite; a program needn't handle non-finite values.
Results may differ from a plain program's by a relative error of at most 0.02.
Values may be sent and summed in bfloat16 or wider, within the bound.
No kernel may reach another device: no remote copies, remote signals or barrier semaphores. Data moves between devices by JAX's collectives and lax.ppermute only.
A program may use at most 128 MiB of HBM per device.

v0:
```python
import jax
import jax.numpy as jnp
from jax import lax
from jax.experimental import pallas as pl
from jax.experimental.pallas import tpu as pltpu
from jax.sharding import PartitionSpec as P


HEADS = 16
LANES = 128
F32 = jnp.float32
BF16 = jnp.bfloat16


def bits_of(size):
    return [1 << i for i in range(size.bit_length() - 1)]


def swap(value, axis, offset):
    size = lax.axis_size(axis)
    return lax.ppermute(value, axis, [(i, i ^ offset) for i in range(size)])


def index_of(axis):
    return lax.axis_index(axis).astype(jnp.uint32)


def tile_width(block):
    return LANES if block % LANES == 0 else block


def as_row(column):
    return jnp.broadcast_to(column, (column.shape[0], LANES)).T[:1]


def as_column(row):
    return jnp.broadcast_to(row, (LANES, row.shape[1])).T[:, :1]


def moments(value):
    mean = jnp.mean(value, axis=1, keepdims=True)
    centred = value - mean
    spread = jnp.sum(centred * centred, axis=1, keepdims=True)
    return centred, jnp.concatenate([as_row(mean), as_row(spread)])


def merge_moments(stats, rows, count):
    means = [stat[:1, rows] for stat in stats]
    mean = sum(means[1:], means[0]) / len(stats)
    spread = sum([stat[1:, rows] for stat in stats[1:]], stats[0][1:, rows])
    gaps = [(m - mean) * (m - mean) for m in means]
    spread = spread + count * sum(gaps[1:], gaps[0])
    return mean, lax.rsqrt(spread / (count * len(stats)) + 1e-05)


def call(body, outs, args, scratch=(), scalars=()):
    space = pl.BlockSpec(memory_space=pltpu.MemorySpace.VMEM)
    scalar = pl.BlockSpec(memory_space=pltpu.MemorySpace.SMEM)
    return pl.pallas_call(
        body,
        out_shape=[jax.ShapeDtypeStruct(shape, dtype) for shape, dtype in outs],
        in_specs=[scalar] * len(scalars) + [space] * len(args),
        out_specs=[space] * len(outs),
        scratch_shapes=list(scratch),
        compiler_params=pltpu.CompilerParams(vmem_limit_bytes=56 * 1024 * 1024),
    )(*scalars, *args)


def attend(mine, blocks, residual, head_dim):
    groups = len(blocks)
    rows, width = blocks[0].shape[1:]
    length = groups * rows
    scale = head_dim ** (-0.5)

    def body(index, *refs):
        parts, rest, (mixed, stat) = refs[:groups], refs[groups : 2 * groups], refs[2 * groups :]
        outs = [[] for _ in parts]
        for low in range(0, width, head_dim):
            cols = slice(low, low + head_dim)
            k = jnp.concatenate([part[1, :, cols] for part in parts])
            v = jnp.concatenate([part[2, :, cols] for part in parts])
            for m, part in enumerate(parts):
                scores = lax.dot_general(
                    part[0, :, cols], k, (((1,), (1,)), ((), ())), preferred_element_type=F32
                )
                scores = scores * scale
                expo = jnp.exp(scores - jnp.max(scores, axis=1, keepdims=True))
                total = jnp.sum(expo, axis=1, keepdims=True)
                summed = jnp.dot(expo.astype(BF16), v, preferred_element_type=F32)
                outs[m].append((summed / total).astype(BF16))
        for m, part in enumerate(rest):
            start = pl.multiple_of((index[0] ^ m) * rows, rows)
            value = part[0].astype(F32) + jnp.concatenate(outs[m], axis=1).astype(F32)
            centred, stat[:, pl.ds(start, rows)] = moments(value)
            mixed[pl.ds(start, rows), :] = centred.astype(BF16)

    return call(
        body, [((length, width), BF16), ((2, length), F32)],
        [*blocks, *residual],
        scalars=[mine.astype(jnp.int32).reshape(1)],
    )


def fill(padded, half, length, width, read):
    tile = tile_width(width)
    for i in range(width // tile):
        padded[i, :half] = jnp.zeros((half, tile), F32)
        padded[i, half + length :] = jnp.zeros((half, tile), F32)
        for low in range(0, length, LANES):
            padded[i, half + low : half + low + LANES] = read(low, i * tile, tile)


def convolve(padded, taps, length, width, places, write, chunk=64):
    tile = tile_width(width)
    for i in range(width // tile):
        cols = slice(i * tile, (i + 1) * tile)

        def step(j, carry, i=i, cols=cols):
            start = pl.multiple_of(j * chunk, chunk)
            total = jnp.zeros((chunk, tile), F32)
            for t, place in enumerate(places):
                total = total + taps[t : t + 1, cols] * padded[i, pl.ds(start + place, chunk)]
            write(start, chunk, cols, total)
            return carry

        lax.fori_loop(0, length // chunk, step, 0)


def gate(parts, stats, gain, w_near, w_far, taps):
    length, block = parts[0].shape
    count = len(parts)
    kernel = taps.shape[0]
    half = kernel // 2
    tile = tile_width(block)

    close, copies = len(w_near), len(w_far)

    def body(index, *refs):
        ins, ws, far = refs[:count], list(refs[count : count + close]), refs[count + close :]
        far, refs = far[:copies], far[copies:]
        stat_refs, refs = refs[:count], refs[count:]
        gain_ref, taps_ref, u_ref, p_ref, y_ref, z_ref, stat, padded = refs[:8]
        if copies:
            whole = refs[8]
            share = far[0].shape[1]
            for offset, ref in enumerate(far):
                start = pl.multiple_of((index[0] ^ offset) * share, share)
                for m in range(count - close):
                    whole[m, pl.ds(start, share), :] = ref[m]
            ws += [whole.at[m] for m in range(count - close)]
        for low in range(0, length, LANES):
            rows = slice(low, low + LANES)
            mean, inv = merge_moments(stat_refs, rows, block)
            shifts = [as_column(ref[:1, rows] - mean) for ref in stat_refs]
            inv = as_column(inv)
            p = jnp.zeros((LANES, 2 * block), F32)
            for m, (part, w) in enumerate(zip(ins, ws)):
                u = (part[rows].astype(F32) + shifts[m]) * inv * gain_ref[m : m + 1]
                u = u.astype(BF16)
                u_ref[rows, m * block : (m + 1) * block] = u
                p = p + jnp.dot(u, w[...], preferred_element_type=F32)
            p_ref[rows] = p
            y_ref[rows] = (p[:, :block] * jax.nn.sigmoid(p[:, block:])).astype(BF16)
        fill(
            padded,
            half,
            length,
            block,
            lambda low, col, size: y_ref[low : low + LANES, col : col + size].astype(F32),
        )

        def write(start, chunk, cols, total):
            z_ref[pl.ds(start, chunk), cols] = total

        convolve(padded, taps_ref, length, block, range(kernel), write)
        for low in range(0, length, LANES):
            rows = slice(low, low + LANES)
            stat[:, rows] = moments(z_ref[rows])[1]

    return call(
        body,
        [
            ((length, count * block), BF16),
            ((length, 2 * block), F32),
            ((length, block), BF16),
            ((length, block), F32),
            ((2, length), F32),
        ],
        [*parts, *w_near, *w_far, *stats, gain, taps],
        [pltpu.VMEM((block // tile, length + 2 * half, tile), F32)]
        + ([pltpu.VMEM((count - close, block, 2 * block), BF16)] if copies else []),
        scalars=[index_of("dp").astype(jnp.int32).reshape(1)],
    )


def swish(z, stats, gain, d_s):
    length, block = z.shape
    count = len(stats)

    def body(z_ref, gain_ref, ds_ref, *refs):
        stat_refs, (s_ref, zhat_ref, e_ref, inv_ref, sums) = refs[:count], refs[count:]
        for low in range(0, length, LANES):
            rows = slice(low, low + LANES)
            mean, inv = merge_moments(stat_refs, rows, block)
            inv_ref[:, rows] = inv
            zhat = (z_ref[rows] - as_column(mean)) * as_column(inv)
            n = zhat * gain_ref[...]
            sgate = jax.nn.sigmoid(n)
            s_ref[:, rows] = (n * sgate).T.astype(BF16)
            e = ds_ref[rows] * sgate * (1.0 + n * (1.0 - sgate)) * gain_ref[...]
            zhat_ref[rows] = zhat
            e_ref[rows] = e
            both = [jnp.sum(e, axis=1, keepdims=True), jnp.sum(e * zhat, axis=1, keepdims=True)]
            sums[:, rows] = jnp.concatenate([as_row(both[0]), as_row(both[1])])

    return call(
        body,
        [
            ((block, length), BF16),
            ((length, block), F32),
            ((length, block), F32),
            ((1, length), F32),
            ((2, length), F32),
        ],
        [z, gain, d_s, *stats],
    )


def ungate(e, zhat, inv, sums, p, taps):
    length, block = e.shape
    kernel = taps.shape[0]
    half = kernel // 2
    tile = tile_width(block)

    count = len(sums)

    def body(e_ref, zhat_ref, inv_ref, p_ref, taps_ref, *refs):
        sum_refs, (dp_ref, dz_ref, padded) = refs[:count], refs[count:]
        for low in range(0, length, LANES):
            rows = slice(low, low + LANES)
            means = sum([ref[:, rows] for ref in sum_refs[1:]], sum_refs[0][:, rows])
            means = means / (block * count)
            mean, mean_z = as_column(means[:1]), as_column(means[1:])
            d_z = (e_ref[rows] - mean - zhat_ref[rows] * mean_z) * as_column(inv_ref[:, rows])
            dz_ref[rows] = d_z.astype(BF16)
        fill(
            padded,
            half,
            length,
            block,
            lambda low, col, size: dz_ref[low : low + LANES, col : col + size].astype(F32),
        )

        def write(start, chunk, cols, total):
            rows = pl.ds(start, chunk)
            first = p_ref[rows, cols]
            sig = jax.nn.sigmoid(p_ref[rows, slice(block + cols.start, block + cols.stop)])
            dp_ref[rows, cols] = (total * sig).astype(BF16)
            dp_ref[rows, slice(block + cols.start, block + cols.stop)] = (
                total * first * sig * (1.0 - sig)
            ).astype(BF16)

        convolve(
            padded, taps_ref, length, block, [2 * half - t for t in range(kernel)], write
        )

    return call(
        body,
        [((length, 2 * block), BF16), ((length, block), BF16)],
        [e, zhat, inv, p, taps, *sums],
        [pltpu.VMEM((block // tile, length + 2 * half, tile), F32)],
    )


def taps_gradient(d_z, y, kernel):
    length, block = y.shape
    half = kernel // 2
    tile = tile_width(block)
    group = 8

    def body(dz_ref, y_ref, out, dz_all, y_pad):
        for ref, padded in ((dz_ref, dz_all), (y_ref, y_pad)):
            fill(
                padded,
                half,
                length,
                block,
                lambda low, col, size, ref=ref: ref[low : low + LANES, col : col + size].astype(F32),
            )
        for i in range(block // tile):

            def step(j, sums, i=i):
                start = pl.multiple_of(j * group, group)
                value = dz_all[i, pl.ds(start + half, group)]
                return tuple(
                    total + value * y_pad[i, pl.ds(start + t, group)]
                    for t, total in enumerate(sums)
                )

            zero = jnp.zeros((group, tile), F32)
            sums = lax.fori_loop(0, length // group, step, (zero,) * kernel)
            out[:, i * tile : (i + 1) * tile] = jnp.concatenate(
                [jnp.sum(total, axis=0, keepdims=True) for total in sums]
            )

    pad = pltpu.VMEM((block // tile, length + 2 * half, tile), F32)
    return call(body, [((kernel, block), F32)], [d_z, y], [pad, pad])[0]


def gather_rows(value, axis, order):
    index = index_of(axis)
    value = value[(None,) * len(order)]
    for bit in order:
        other = swap(value, axis, bit)
        upper = (index // bit) % 2 == 1
        place = len(order) - bit.bit_length()
        value = jnp.concatenate(
            [jnp.where(upper, other, value), jnp.where(upper, value, other)], axis=place
        )
    return value.reshape((lax.axis_size(axis),) + value.shape[len(order) :])


def tree(value, axis, order):
    parts = {0: value}
    for bit in order:
        parts |= {offset ^ bit: swap(part, axis, bit) for offset, part in parts.items()}
    return parts


def rows_in_place(jobs, widths, axis, into=()):
    count, given = len(jobs), len(into)
    total = lax.axis_size(axis) * jobs[0][0].shape[0]

    def body(index, *refs):
        ins = refs[:count]
        outs = refs[count + given : count + given + len(widths)]
        wides, sem = refs[count + given + len(widths) : -1], refs[-1]
        copies = []
        for ref, wide, (_, offset, spans) in zip(ins, wides, jobs):
            share = ref.shape[0]
            wide[...] = ref[...].astype(F32)
            start = pl.multiple_of((index[0] ^ offset) * share, share)
            for which, low, high, place in spans:
                copy = pltpu.make_async_copy(
                    wide.at[:, low:high],
                    outs[which].at[pl.ds(start, share), place : place + high - low],
                    sem.at[len(copies)],
                )
                copy.start()
                copies.append(copy)
        for copy in copies:
            copy.wait()

    space = pl.BlockSpec(memory_space=pltpu.MemorySpace.VMEM)
    whole = pl.BlockSpec(memory_space=pl.ANY)
    return pl.pallas_call(
        body,
        out_shape=[jax.ShapeDtypeStruct((total, width), F32) for width in widths],
        in_specs=[pl.BlockSpec(memory_space=pltpu.MemorySpace.SMEM)]
        + [space] * count
        + [whole] * given,
        out_specs=[whole] * len(widths),
        scratch_shapes=[pltpu.VMEM(array.shape, F32) for array, _, _ in jobs]
        + [pltpu.SemaphoreType.DMA((sum(len(spans) for _, _, spans in jobs),))],
        input_output_aliases={count + 1 + j: j for j in range(given)},
        compiler_params=pltpu.CompilerParams(vmem_limit_bytes=56 * 1024 * 1024),
    )(index_of(axis).astype(jnp.int32).reshape(1), *[job[0] for job in jobs], *into)


def gather_both(glu, out, near, far):
    share, wide = glu.shape
    width = out.shape[1]
    cut = width // 2
    both = jnp.concatenate([glu, out[:, :cut]], axis=1)
    middle = (wide + cut) // 2
    if share % 16 == 0 and middle % LANES == 0 and middle <= wide:
        one = tree(both[:, :middle], "dp", near)
        two = tree(both[:, middle:], "dp", near)
        short = tree(out[:, cut:], "dp", far)
        spans = [(0, 0, middle, 0)], [
            (0, 0, wide - middle, middle),
            (1, wide - middle, middle, 0),
        ]
        jobs = [(part, o, spans[i]) for i, parts in enumerate((one, two)) for o, part in parts.items()]
        jobs += [(part, o, [(1, 0, cut, cut)]) for o, part in short.items()]
        first = [0] + near[:2]
        early = [job for job in jobs[: 2 * len(one)] if job[1] in first]
        early += [job for job in jobs[2 * len(one) :] if job[1] in (0, far[0])]
        rest = [job for job in jobs if not any(job is other for other in early)]
        into = rows_in_place(early, (wide, width), "dp")
        return rows_in_place(rest, (wide, width), "dp", into)
    long, short = both, out[:, cut:]
    long = gather_rows(long, "dp", near).reshape(-1, wide + cut).astype(F32)
    short = gather_rows(short, "dp", far).reshape(-1, width - cut).astype(F32)
    return long[:, :wide], jnp.concatenate([long[:, wide:], short], axis=1)


class Halving:
    def __init__(self, value, axis, order):
        self.axis, self.order = axis, list(order)
        self.left = sorted(order, reverse=True)
        self.value = value.reshape((2,) * len(order) + value.shape[1:])
        self.give = None

    def split(self):
        bit = self.order.pop(0)
        place = self.left.index(bit)
        self.left.remove(bit)
        mine = (index_of(self.axis) // bit) % 2
        self.bit = bit
        self.give = lax.dynamic_index_in_dim(self.value, 1 - mine, place, keepdims=False)
        self.give = self.give.astype(BF16)
        self.value = lax.dynamic_index_in_dim(self.value, mine, place, keepdims=False)

    def join(self):
        got = swap(self.give, self.axis, self.bit)
        self.value = self.value.astype(F32) + got.astype(F32)
        self.give = None


def together(items, *others):
    fixed = lax.optimization_barrier((tuple(item.give for item in items), others))
    for item, give in zip(items, fixed[0]):
        item.give = give
    return fixed[1]


def orders(size):
    bits = bits_of(size)
    return bits, bits[1:] + bits[:1]


def whole_step(frames, query, keys, values, norm_gain, conv_gain, w_glu, taps, w_out, cotangent):
    groups = lax.axis_size("tm")
    copies = lax.axis_size("dp")
    mine = index_of("tm")
    rows, width = frames.shape[1:]
    length = rows * groups
    block = width // groups
    share = block // copies
    tm_bits = bits_of(lax.axis_size("tm"))
    offsets = list(range(groups))
    near, far = orders(lax.axis_size("dp"))

    def columns(arr, owner, low=0):
        return lax.dynamic_slice_in_dim(arr, owner * block + low, block, arr.ndim - 1)

    norm_all = jnp.concatenate([columns(norm_gain[None], mine ^ o) for o in offsets])
    conv_own = columns(conv_gain[None], mine)
    taps_own = columns(taps, mine)

    def glu_columns(arr, owner):
        return jnp.concatenate([columns(arr, owner), columns(arr, owner, width)], axis=1)

    distant = [o for o in offsets if o > 1]
    if distant:
        place = index_of("dp") * share
        w_share = lax.dynamic_slice_in_dim(w_glu, place, share, 0)
        fetched = jnp.stack([swap(glu_columns(w_share, mine ^ o), "tm", o) for o in distant])

    def exchange(arrays):
        blocks = []
        for m in range(groups):
            piece = jnp.concatenate([columns(arr, mine ^ m) for arr in arrays])
            blocks.append(piece if m == 0 else swap(piece, "tm", m))
        return blocks

    blocks = exchange([query, keys, values])
    residual = exchange([frames])
    w_parts = {0: glu_columns(w_glu, mine), 1: swap(glu_columns(w_glu, mine ^ 1), "tm", 1)}

    w_far = {}
    if distant and share % 16 == 0:
        w_far = tree(fetched, "dp", near[::-1])
    elif distant:
        spread = gather_rows(fetched, "dp", near[::-1])
        for i, offset in enumerate(distant):
            w_parts[offset] = spread[:, i].reshape(block, 2 * block)

    mixed, stat_u = attend(mine, blocks, residual, width // HEADS)
    stats_u = tree(stat_u, "tm", tm_bits)
    parts = {0: mixed}
    for bit in reversed(tm_bits):
        parts |= {offset ^ bit: swap(part, "tm", bit) for offset, part in parts.items()}
    cot_all = gather_rows(cotangent[0], "tm", tm_bits[::-1]).reshape(length, width)
    d_s = lax.dot_general(cot_all, w_out, (((1,), (1,)), ((), ())), preferred_element_type=F32)

    last = parts[groups - 1]
    d_s, parts[groups - 1] = lax.optimization_barrier((d_s, last))
    u_all, p_own, y_rows, z_rows, stat_z = gate(
        [parts[o] for o in offsets],
        [stats_u[o] for o in offsets],
        norm_all,
        list(w_parts.values()),
        [w_far[o] for o in range(len(w_far))],
        taps_own,
    )
    stats_z = tree(stat_z, "tm", tm_bits)
    s_turned, zhat, e_rows, inv, sums = swish(z_rows, list(stats_z.values()), conv_own, d_s)
    contract = (((0,), (0,)), ((), ()))
    middle = width // 2
    out_term = jnp.dot(s_turned, cot_all, preferred_element_type=F32)
    out_term = out_term.reshape(copies, share, width)
    outs = [Halving(out_term[..., :middle], "dp", near), Halving(out_term[..., middle:], "dp", far)]
    steps = len(near)
    for item in outs:
        item.split()
    (sums,) = together(outs, sums)
    for item in outs:
        item.join()

    sums = list(tree(sums, "tm", tm_bits).values())
    d_p, d_z = ungate(e_rows, zhat, inv, sums, p_own, taps_own)
    if steps > 1:
        for item in outs:
            item.split()
        (d_p,) = together(outs, d_p)
        for item in outs:
            item.join()

    glu_term = lax.dot_general(u_all, d_p, contract, preferred_element_type=F32)
    glu_term = glu_term.reshape(groups, copies, share, 2 * block).transpose(1, 0, 2, 3)
    glus = [Halving(glu_term[..., :block], "dp", near), Halving(glu_term[..., block:], "dp", far)]
    for item in glus:
        item.split()
    d_z, y_rows = together(glus, d_z, y_rows)
    taps_sum = taps_gradient(d_z, y_rows, taps.shape[0])
    for item in glus:
        item.join()
    for i in range(1, steps):
        for item in glus:
            item.split()
        (taps_sum,) = together(glus[:1], taps_sum)
        if i + 1 < steps:
            for item in outs:
                item.split()
            together(glus[:1] + outs)
            for item in outs:
                item.join()
        taps_sum = taps_sum + swap(taps_sum, "dp", near[i - 1])
        for item in glus:
            item.join()

    pieces = []
    for item in glus:
        part = item.value.astype(BF16)
        got = jnp.stack([part[0]] + [swap(part[o], "tm", o) for o in offsets[1:]])
        ordered = [
            lax.dynamic_index_in_dim(got, mine ^ g, 0, keepdims=False) for g in range(groups)
        ]
        pieces += ordered
    out_piece = jnp.concatenate([item.value.astype(BF16) for item in outs], axis=1)
    glu_piece = jnp.concatenate(pieces, axis=1)
    (taps_sum, glu_piece) = lax.optimization_barrier((taps_sum, glu_piece))
    taps_sum = taps_sum + swap(taps_sum, "dp", near[-1])
    glu_grad, out_grad = gather_both(glu_piece, out_piece, near[::-1], far[::-1])
    return (glu_grad, taps_sum, out_grad)


def solution(mesh):
    return jax.shard_map(
        whole_step,
        mesh=mesh,
        in_specs=(
            P("dp", "tm", None),
            P("dp", "tm", None),
            P("dp", "tm", None),
            P("dp", "tm", None),
            P(),
            P(),
            P("tm", None),
            P(),
            P("tm", None),
            P("dp", "tm", None),
        ),
        out_specs=(P("tm", None), P(None, "tm"), P("tm", None)),
        check_vma=False,
    )
```

profile of v0, /device:TPU:0, one launch (start us, length us, event | category | flops | bytes accessed | tf_op | source)
XLA Modules:
  0.0 225.1 jit_solution(9633883841246089215)
XLA Ops:
  23.4 8.4 %collective-permute-done.4.refs_6_ = bf16[1,128,384]{2,1,0:T(8,128)(2,1)S(1)} collective-permute-done((bf16[1,128,384]{2,1,0:T(8,128)(2,1)S(1)}, bf16[1,128,384]{2,1,0:T(8,128)(2,1)S(1)}, u32[]{:S(2)}, u32[]{:S(2)}) %collective-permute-start.4) | collective-permute-done | bytes 98336 | tf_op jit(solution)/shard_map/ppermute | solution.py:21
  34.2 7.5 %shard_map.121 = (bf16[512,384]{1,0:T(8,128)(2,1)}, f32[2,512]{1,0:T(2,128)}) custom-call(s32[1]{0:T(128)} %bitcast.1.index, bf16[3,128,384]{2,1,0:T(8,128)(2,1)} %pad_maximum_fusion.4.refs_0_, bf16[3,128,384]{2,1,0:T(8,128)(2,1)} %collective-permute-done.refs_1_, bf16[3,128,384]{2,1,0:T(8,128)(2,1)} %collective-permute-done.1.refs_2_, ...), custom_call_target="tpu_custom_call" | custom-call | tf_op jit(solution)/shard_map/pallas_call | solution.py:59
  43.5 2.7 %collective-permute-start.17 = (bf16[2,48,768]{2,1,0:T(8,128)(2,1)S(1)}, bf16[2,48,768]{2,1,0:T(8,128)(2,1)}, u32[]{:S(2)}, u32[]{:S(2)}) collective-permute-start(bf16[2,48,768]{2,1,0:T(8,128)(2,1)S(1)} %pad_maximum_fusion.9.refs_6_), channel_id=1, source_target_pairs={{0,16},{4,20},{8,24},{12,28},{16,0},{20,4},{24,8},{28,12},{1,17},{... | collective-permute-start | bytes 442376 | tf_op jit(solution)/shard_map/ppermute | solution.py:21
  50.6 2.8 %collective-permute-done.17.refs_10_ = bf16[2,48,768]{2,1,0:T(8,128)(2,1)} collective-permute-done((bf16[2,48,768]{2,1,0:T(8,128)(2,1)S(1)}, bf16[2,48,768]{2,1,0:T(8,128)(2,1)}, u32[]{:S(2)}, u32[]{:S(2)}) %collective-permute-start.17) | collective-permute-done | bytes 147488 | tf_op jit(solution)/shard_map/ppermute | solution.py:21
  67.9 3.2 %collective-permute-done.16.refs_9_ = bf16[2,48,768]{2,1,0:T(8,128)(2,1)S(1)} collective-permute-done((bf16[2,48,768]{2,1,0:T(8,128)(2,1)S(1)}, bf16[2,48,768]{2,1,0:T(8,128)(2,1)S(1)}, u32[]{:S(2)}, u32[]{:S(2)}) %collective-permute-start.16) | collective-permute-done | bytes 147488 | tf_op jit(solution)/shard_map/ppermute | solution.py:21
  73.8 8.4 %shard_map.122 = (bf16[512,1536]{1,0:T(8,128)(2,1)}, f32[512,768]{1,0:T(8,128)}, bf16[512,384]{1,0:T(8,128)(2,1)}, f32[512,384]{1,0:T(8,128)}, f32[2,512]{1,0:T(2,128)}) custom-call(s32[1]{0:T(128)} %bitcast.index, bf16[512,384]{1,0:T(8,128)(2,1)} %get-tuple-element.42.refs_0_, bf16[512,384]{1,0:T(8,128)(2,1)} %copy-done.11, ...), custom_call_target="tpu_custom_call" | custom-call | tf_op jit(solution)/shard_map/pallas_call | solution.py:59
  87.8 4.0 %shard_map.123 = (bf16[384,512]{1,0:T(8,128)(2,1)}, f32[512,384]{1,0:T(8,128)}, f32[512,384]{1,0:T(8,128)}, f32[1,512]{1,0:T(1,128)}, f32[2,512]{1,0:T(2,128)}) custom-call(f32[512,384]{1,0:T(8,128)} %get-tuple-element.46.z_ref, f32[1,384]{1,0:T(1,128)} %dynamic_slice.227.gain_ref, f32[512,384]{1,0:T(8,128)} %fusion.22.ds_ref, ...), custom_call_target="tpu_custom_call" | custom-call | tf_op jit(solution)/shard_map/pallas_call | solution.py:59
  100.9 5.9 %shard_map.124 = (bf16[512,768]{1,0:T(8,128)(2,1)}, bf16[512,384]{1,0:T(8,128)(2,1)}) custom-call(f32[512,384]{1,0:T(8,128)} %get-tuple-element.53.e_ref, f32[512,384]{1,0:T(8,128)} %get-tuple-element.54.zhat_ref, f32[1,512]{1,0:T(1,128)} %get-tuple-element.55.inv_ref, f32[512,768]{1,0:T(8,128)} %get-tuple-element.56.p_ref, ...), custom_call_target="tpu_custom_call" | custom-call | tf_op jit(solution)/shard_map/pallas_call | solution.py:59
  108.9 2.9 %collective-permute-start.34 = (bf16[2,48,768]{2,1,0:T(8,128)(2,1)S(1)}, bf16[2,48,768]{2,1,0:T(8,128)(2,1)}, u32[]{:S(2)}, u32[]{:S(2)}) collective-permute-start(bf16[2,48,768]{2,1,0:T(8,128)(2,1)S(1)} %fusion.9), channel_id=1, source_target_pairs={{0,16},{4,20},{8,24},{12,28},{16,0},{20,4},{24,8},{28,12},{1,17},{... | collective-permute-start | bytes 442376 | tf_op jit(solution)/shard_map/ppermute | solution.py:21
  116.0 6.0 %shard_map.125 = f32[32,384]{1,0:T(8,128)} custom-call(bf16[512,384]{1,0:T(8,128)(2,1)} %get-tuple-element.63.dz_ref, bf16[512,384]{1,0:T(8,128)(2,1)} %get-tuple-element.64.y_ref), custom_call_target="tpu_custom_call" | custom-call | tf_op jit(solution)/shard_map/pallas_call | solution.py:59
  123.0 5.4 %collective-permute-done.32 = bf16[2,2,4,48,384]{4,3,2,1,0:T(8,128)(2,1)} collective-permute-done((bf16[2,2,4,48,384]{4,3,2,1,0:T(8,128)(2,1)S(1)}, bf16[2,2,4,48,384]{4,3,2,1,0:T(8,128)(2,1)}, u32[]{:S(2)}, u32[]{:S(2)}) %collective-permute-start.32) | collective-permute-done | bytes 589856 | tf_op jit(solution)/shard_map/ppermute | solution.py:21
  133.4 2.7 %collective-permute-start.43 = (bf16[2,4,48,384]{3,2,1,0:T(8,128)(2,1)S(1)}, bf16[2,4,48,384]{3,2,1,0:T(8,128)(2,1)S(1)}, u32[]{:S(2)}, u32[]{:S(2)}) collective-permute-start(bf16[2,4,48,384]{3,2,1,0:T(8,128)(2,1)S(1)} %fusion.3), channel_id=1, source_target_pairs={{0,16},{4,20},{8,24},{12,28},{16,0},{20,4},{24,8},{28,12},{1,17},{... | collective-permute-start | bytes 884744 | tf_op jit(solution)/shard_map/ppermute | solution.py:21
  137.3 2.5 %collective-permute-start.64 = (bf16[48,768]{1,0:T(8,128)(2,1)S(1)}, bf16[48,768]{1,0:T(8,128)(2,1)S(1)}, u32[]{:S(2)}, u32[]{:S(2)}) collective-permute-start(bf16[48,768]{1,0:T(8,128)(2,1)S(1)} %fusion.12.refs_6_), channel_id=1, source_target_pairs={{0,16},{4,20},{8,24},{12,28},{16,0},{20,4},{24,8},{28,12},{1,17},{... | collective-permute-start | bytes 221192 | tf_op jit(solution)/shard_map/ppermute | solution.py:21
  139.8 5.5 %collective-permute-done.35 = bf16[2,4,48,384]{3,2,1,0:T(8,128)(2,1)S(1)} collective-permute-done((bf16[2,4,48,384]{3,2,1,0:T(8,128)(2,1)S(1)}, bf16[2,4,48,384]{3,2,1,0:T(8,128)(2,1)S(1)}, u32[]{:S(2)}, u32[]{:S(2)}) %collective-permute-start.35) | collective-permute-done | bytes 294944 | tf_op jit(solution)/shard_map/ppermute | solution.py:21
  147.9 7.4 %collective-permute-done.43 = bf16[2,4,48,384]{3,2,1,0:T(8,128)(2,1)S(1)} collective-permute-done((bf16[2,4,48,384]{3,2,1,0:T(8,128)(2,1)S(1)}, bf16[2,4,48,384]{3,2,1,0:T(8,128)(2,1)S(1)}, u32[]{:S(2)}, u32[]{:S(2)}) %collective-permute-start.43) | collective-permute-done | bytes 294944 | tf_op jit(solution)/shard_map/ppermute | solution.py:21
  176.4 7.9 %collective-permute-done.70.refs_15_ = bf16[48,768]{1,0:T(8,128)(2,1)S(1)} collective-permute-done((bf16[48,768]{1,0:T(8,128)(2,1)S(1)}, bf16[48,768]{1,0:T(8,128)(2,1)S(1)}, u32[]{:S(2)}, u32[]{:S(2)}) %collective-permute-start.70) | collective-permute-done | bytes 73760 | tf_op jit(solution)/shard_map/ppermute | solution.py:21
  184.3 2.6 %collective-permute-start.71 = (f32[32,384]{1,0:T(8,128)S(1)}, f32[32,384]{1,0:T(8,128)S(1)}, u32[]{:S(2)}, u32[]{:S(2)}) collective-permute-start(f32[32,384]{1,0:T(8,128)S(1)} %add.97), channel_id=1, source_target_pairs={{0,16},{4,20},{8,24},{12,28},{16,0},{20,4},{24,8},{28,12},{1,17},{... | collective-permute-start | bytes 147464 | tf_op jit(solution)/shard_map/ppermute | solution.py:21
  186.9 4.4 %collective-permute-done.71 = f32[32,384]{1,0:T(8,128)S(1)} collective-permute-done((f32[32,384]{1,0:T(8,128)S(1)}, f32[32,384]{1,0:T(8,128)S(1)}, u32[]{:S(2)}, u32[]{:S(2)}) %collective-permute-start.71) | collective-permute-done | bytes 49184 | tf_op jit(solution)/shard_map/ppermute | solution.py:21
  195.9 2.9 %collective-permute-done.52.refs_2_ = bf16[48,1920]{1,0:T(8,128)(2,1)S(1)} collective-permute-done((bf16[48,1920]{1,0:T(8,128)(2,1)S(1)}, bf16[48,1920]{1,0:T(8,128)(2,1)S(1)}, u32[]{:S(2)}, u32[]{:S(2)}) %collective-permute-start.52) | collective-permute-done | bytes 184352 | tf_op jit(solution)/shard_map/ppermute | solution.py:21
  200.9 2.5 %collective-permute-done.61.refs_8_ = bf16[48,1920]{1,0:T(8,128)(2,1)S(1)} collective-permute-done((bf16[48,1920]{1,0:T(8,128)(2,1)S(1)}, bf16[48,1920]{1,0:T(8,128)(2,1)S(1)}, u32[]{:S(2)}, u32[]{:S(2)}) %collective-permute-start.61) | collective-permute-done | bytes 184352 | tf_op jit(solution)/shard_map/ppermute | solution.py:21
  206.6 2.9 %shard_map.126 = (f32[384,3072]{1,0:T(8,128)}, f32[384,1536]{1,0:T(8,128)}) custom-call(s32[1]{0:T(128)} %bitcast.index, bf16[48,1920]{1,0:T(8,128)(2,1)} %copy-done.5, bf16[48,1920]{1,0:T(8,128)(2,1)} %copy-done.19, bf16[48,1920]{1,0:T(8,128)(2,1)} %copy-done.20, bf16[48,1920]{1,0:T(8,128)(2,1)} %copy-done.4, bf16[48,1920]{1,0:T(8,128)(2,1)} %copy-done.18, ...), custom_call_target="tpu_custom_call" | custom-call | tf_op jit(solution)/shard_map/pallas_call | solution.py:356
  209.6 5.6 %collective-permute-done.53.refs_3_ = bf16[48,1920]{1,0:T(8,128)(2,1)S(1)} collective-permute-done((bf16[48,1920]{1,0:T(8,128)(2,1)S(1)}, bf16[48,1920]{1,0:T(8,128)(2,1)S(1)}, u32[]{:S(2)}, u32[]{:S(2)}) %collective-permute-start.53) | collective-permute-done | bytes 184352 | tf_op jit(solution)/shard_map/ppermute | solution.py:21
  215.2 3.0 %collective-permute-done.62.refs_9_ = bf16[48,1920]{1,0:T(8,128)(2,1)S(1)} collective-permute-done((bf16[48,1920]{1,0:T(8,128)(2,1)S(1)}, bf16[48,1920]{1,0:T(8,128)(2,1)S(1)}, u32[]{:S(2)}, u32[]{:S(2)}) %collective-permute-start.62) | collective-permute-done | bytes 184352 | tf_op jit(solution)/shard_map/ppermute | solution.py:21
  220.8 4.1 %shard_map.127 = (f32[384,3072]{1,0:T(8,128)}, f32[384,1536]{1,0:T(8,128)}) custom-call(s32[1]{0:T(128)} %bitcast.index, bf16[48,1920]{1,0:T(8,128)(2,1)} %copy-done.25, bf16[48,1920]{1,0:T(8,128)(2,1)} %copy-done.22, bf16[48,1920]{1,0:T(8,128)(2,1)} %copy-done.27, bf16[48,1920]{1,0:T(8,128)(2,1)} %copy-done.28, ...), custom_call_target="tpu_custom_call", output_to_operand_aliasing={{0}: (17, {}), {1}: (18, {})} | custom-call | tf_op jit(solution)/shard_map/pallas_call | solution.py:356
  (318 shorter events, 112.3 us)
Async XLA Ops:
  2.6 14.9 %collective-permute-start.5 = (bf16[1,128,384]{2,1,0:T(8,128)(2,1)}, bf16[1,128,384]{2,1,0:T(8,128)(2,1)}, u32[]{:S(2)}, u32[]{:S(2)}) collective-permute-start(bf16[1,128,384]{2,1,0:T(8,128)(2,1)} %get-tuple-element.97), channel_id=1, source_target_pairs={{0,3},{1,2},{2,1},{3,0},{4,7},{5,6},{6,5},{7,4},{8,11},{9,10},{10,... | collective-permute-start | bytes 294920 | tf_op jit(solution)/shard_map/ppermute | solution.py:21
  7.6 26.2 %collective-permute-start.1 = (bf16[3,128,384]{2,1,0:T(8,128)(2,1)}, bf16[3,128,384]{2,1,0:T(8,128)(2,1)}, u32[]{:S(2)}, u32[]{:S(2)}) collective-permute-start(bf16[3,128,384]{2,1,0:T(8,128)(2,1)} %pad_maximum_fusion.6), channel_id=1, source_target_pairs={{0,2},{1,3},{2,0},{3,1},{4,6},{5,7},{6,4},{7,5},{8,10},{9,11},{10,... | collective-permute-start | bytes 884744 | tf_op jit(solution)/shard_map/ppermute | solution.py:21
  9.8 24.4 %collective-permute-start = (bf16[3,128,384]{2,1,0:T(8,128)(2,1)}, bf16[3,128,384]{2,1,0:T(8,128)(2,1)}, u32[]{:S(2)}, u32[]{:S(2)}) collective-permute-start(bf16[3,128,384]{2,1,0:T(8,128)(2,1)} %pad_maximum_fusion.5), channel_id=1, source_target_pairs={{0,1},{1,0},{2,3},{3,2},{4,5},{5,4},{6,7},{7,6},{8,9},{9,8},{10,11... | collective-permute-start | bytes 884744 | tf_op jit(solution)/shard_map/ppermute | solution.py:21
  10.7 23.5 %collective-permute-start.2 = (bf16[3,128,384]{2,1,0:T(8,128)(2,1)}, bf16[3,128,384]{2,1,0:T(8,128)(2,1)}, u32[]{:S(2)}, u32[]{:S(2)}) collective-permute-start(bf16[3,128,384]{2,1,0:T(8,128)(2,1)} %pad_maximum_fusion.7), channel_id=1, source_target_pairs={{0,3},{1,2},{2,1},{3,0},{4,7},{5,6},{6,5},{7,4},{8,11},{9,10},{10,... | collective-permute-start | bytes 884744 | tf_op jit(solution)/shard_map/ppermute | solution.py:21
  17.4 36.5 %collective-permute-start.9 = (bf16[2,1,128,1536]{3,2,1,0:T(8,128)(2,1)S(1)}, bf16[2,1,128,1536]{3,2,1,0:T(8,128)(2,1)}, u32[]{:S(2)}, u32[]{:S(2)}) collective-permute-start(bf16[2,1,128,1536]{3,2,1,0:T(8,128)(2,1)S(1)} %pad_maximum_fusion.1), channel_id=1, source_target_pairs={{0,1},{1,0},{2,3},{3,2},{4,5},{5,4},{6,7},{7,6},{8,9},{9,8},{10,11... | collective-permute-start | bytes 2359304 | tf_op jit(solution)/shard_map/ppermute | solution.py:21
  55.7 17.1 %collective-permute-start.11 = (bf16[384,768]{1,0:T(8,128)(2,1)S(1)}, bf16[384,768]{1,0:T(8,128)(2,1)S(1)}, u32[]{:S(2)}, u32[]{:S(2)}) collective-permute-start(bf16[384,768]{1,0:T(8,128)(2,1)S(1)} %copy-done.7), channel_id=1, source_target_pairs={{0,1},{1,0},{2,3},{3,2},{4,5},{5,4},{6,7},{7,6},{8,9},{9,8},{10,11... | collective-permute-start | bytes 1769480 | tf_op jit(solution)/shard_map/ppermute | solution.py:21
  57.2 15.6 %collective-permute-start.6 = (bf16[512,384]{1,0:T(8,128)(2,1)S(1)}, bf16[512,384]{1,0:T(8,128)(2,1)S(1)}, u32[]{:S(2)}, u32[]{:S(2)}) collective-permute-start(bf16[512,384]{1,0:T(8,128)(2,1)S(1)} %copy-done.9), channel_id=1, source_target_pairs={{0,1},{1,0},{2,3},{3,2},{4,5},{5,4},{6,7},{7,6},{8,9},{9,8},{10,11... | collective-permute-start | bytes 1179656 | tf_op jit(solution)/shard_map/ppermute | solution.py:21
  93.9 12.9 %collective-permute-start.27 = (bf16[2,2,48,768]{3,2,0,1:T(8,128)(2,1)S(1)}, bf16[2,2,48,768]{3,2,0,1:T(8,128)(2,1)S(1)}, u32[]{:S(2)}, u32[]{:S(2)}) collective-permute-start(bf16[2,2,48,768]{3,2,0,1:T(8,128)(2,1)S(1)} %fusion.4), channel_id=1, source_target_pairs={{0,4},{4,0},{8,12},{12,8},{16,20},{20,16},{24,28},{28,24},{1,5},{5... | collective-permute-start | bytes 884744 | tf_op jit(solution)/shard_map/ppermute | solution.py:21
  107.7 14.3 %collective-permute-start.33 = (bf16[2,48,768]{2,1,0:T(8,128)(2,1)}, bf16[2,48,768]{2,1,0:T(8,128)(2,1)S(1)}, u32[]{:S(2)}, u32[]{:S(2)}) collective-permute-start(bf16[2,48,768]{2,1,0:T(8,128)(2,1)} %fusion.8), channel_id=1, source_target_pairs={{0,8},{4,12},{8,0},{12,4},{16,24},{20,28},{24,16},{28,20},{1,9},{5... | collective-permute-start | bytes 442376 | tf_op jit(solution)/shard_map/ppermute | solution.py:21
  108.9 13.2 %collective-permute-start.34 = (bf16[2,48,768]{2,1,0:T(8,128)(2,1)S(1)}, bf16[2,48,768]{2,1,0:T(8,128)(2,1)}, u32[]{:S(2)}, u32[]{:S(2)}) collective-permute-start(bf16[2,48,768]{2,1,0:T(8,128)(2,1)S(1)} %fusion.9), channel_id=1, source_target_pairs={{0,16},{4,20},{8,24},{12,28},{16,0},{20,4},{24,8},{28,12},{1,17},{... | collective-permute-start | bytes 442376 | tf_op jit(solution)/shard_map/ppermute | solution.py:21
  114.3 14.2 %collective-permute-start.32 = (bf16[2,2,4,48,384]{4,3,2,1,0:T(8,128)(2,1)S(1)}, bf16[2,2,4,48,384]{4,3,2,1,0:T(8,128)(2,1)}, u32[]{:S(2)}, u32[]{:S(2)}) collective-permute-start(bf16[2,2,4,48,384]{4,3,2,1,0:T(8,128)(2,1)S(1)} %fusion), channel_id=1, source_target_pairs={{0,4},{4,0},{8,12},{12,8},{16,20},{20,16},{24,28},{28,24},{1,5},{5... | collective-permute-start | bytes 1769480 | tf_op jit(solution)/shard_map/ppermute | solution.py:21
  114.9 18.3 %collective-permute-start.42 = (bf16[2,2,4,48,384]{4,3,2,1,0:T(8,128)(2,1)S(1)}, bf16[2,2,4,48,384]{4,3,2,1,0:T(8,128)(2,1)S(1)}, u32[]{:S(2)}, u32[]{:S(2)}) collective-permute-start(bf16[2,2,4,48,384]{4,3,2,1,0:T(8,128)(2,1)S(1)} %fusion.1), channel_id=1, source_target_pairs={{0,8},{4,12},{8,0},{12,4},{16,24},{20,28},{24,16},{28,20},{1,9},{5... | collective-permute-start | bytes 1769480 | tf_op jit(solution)/shard_map/ppermute | solution.py:21
  132.2 13.0 %collective-permute-start.35 = (bf16[2,4,48,384]{3,2,1,0:T(8,128)(2,1)S(1)}, bf16[2,4,48,384]{3,2,1,0:T(8,128)(2,1)S(1)}, u32[]{:S(2)}, u32[]{:S(2)}) collective-permute-start(bf16[2,4,48,384]{3,2,1,0:T(8,128)(2,1)S(1)} %fusion.2), channel_id=1, source_target_pairs={{0,8},{4,12},{8,0},{12,4},{16,24},{20,28},{24,16},{28,20},{1,9},{5... | collective-permute-start | bytes 884744 | tf_op jit(solution)/shard_map/ppermute | solution.py:21
  133.4 21.8 %collective-permute-start.43 = (bf16[2,4,48,384]{3,2,1,0:T(8,128)(2,1)S(1)}, bf16[2,4,48,384]{3,2,1,0:T(8,128)(2,1)S(1)}, u32[]{:S(2)}, u32[]{:S(2)}) collective-permute-start(bf16[2,4,48,384]{3,2,1,0:T(8,128)(2,1)S(1)} %fusion.3), channel_id=1, source_target_pairs={{0,16},{4,20},{8,24},{12,28},{16,0},{20,4},{24,8},{28,12},{1,17},{... | collective-permute-start | bytes 884744 | tf_op jit(solution)/shard_map/ppermute | solution.py:21
  136.2 27.3 %collective-permute-start.65 = (bf16[48,768]{1,0:T(8,128)(2,1)S(1)}, bf16[48,768]{1,0:T(8,128)(2,1)S(1)}, u32[]{:S(2)}, u32[]{:S(2)}) collective-permute-start(bf16[48,768]{1,0:T(8,128)(2,1)S(1)} %fusion.12.refs_6_), channel_id=1, source_target_pairs={{0,4},{4,0},{8,12},{12,8},{16,20},{20,16},{24,28},{28,24},{1,5},{5... | collective-permute-start | bytes 221192 | tf_op jit(solution)/shard_map/ppermute | solution.py:21
  137.3 26.3 %collective-permute-start.64 = (bf16[48,768]{1,0:T(8,128)(2,1)S(1)}, bf16[48,768]{1,0:T(8,128)(2,1)S(1)}, u32[]{:S(2)}, u32[]{:S(2)}) collective-permute-start(bf16[48,768]{1,0:T(8,128)(2,1)S(1)} %fusion.12.refs_6_), channel_id=1, source_target_pairs={{0,16},{4,20},{8,24},{12,28},{16,0},{20,4},{24,8},{28,12},{1,17},{... | collective-permute-start | bytes 221192 | tf_op jit(solution)/shard_map/ppermute | solution.py:21
  145.4 12.4 %collective-permute-start.38 = (bf16[4,48,384]{2,1,0:T(8,128)(2,1)S(1)}, bf16[4,48,384]{2,1,0:T(8,128)(2,1)S(1)}, u32[]{:S(2)}, u32[]{:S(2)}) collective-permute-start(bf16[4,48,384]{2,1,0:T(8,128)(2,1)S(1)} %fusion.10), channel_id=1, source_target_pairs={{0,16},{4,20},{8,24},{12,28},{16,0},{20,4},{24,8},{28,12},{1,17},{... | collective-permute-start | bytes 442376 | tf_op jit(solution)/shard_map/ppermute | solution.py:21
  168.0 23.9 %collective-permute-start.60 = (bf16[48,1920]{1,0:T(8,128)(2,1)S(1)}, bf16[48,1920]{1,0:T(8,128)(2,1)S(1)}, u32[]{:S(2)}, u32[]{:S(2)}) collective-permute-start(bf16[48,1920]{1,0:T(8,128)(2,1)S(1)} %get-tuple-element.113.refs_3_), channel_id=1, source_target_pairs={{0,8},{4,12},{8,0},{12,4},{16,24},{20,28},{24,16},{28,20},{1,9},{5... | collective-permute-start | bytes 552968 | tf_op jit(solution)/shard_map/ppermute | solution.py:21
  168.7 23.7 %collective-permute-start.58 = (bf16[48,1920]{1,0:T(8,128)(2,1)S(1)}, bf16[48,1920]{1,0:T(8,128)(2,1)S(1)}, u32[]{:S(2)}, u32[]{:S(2)}) collective-permute-start(bf16[48,1920]{1,0:T(8,128)(2,1)S(1)} %get-tuple-element.113.refs_3_), channel_id=1, source_target_pairs={{0,4},{4,0},{8,12},{12,8},{16,20},{20,16},{24,28},{28,24},{1,5},{5... | collective-permute-start | bytes 552968 | tf_op jit(solution)/shard_map/ppermute | solution.py:21
  171.3 22.6 %collective-permute-start.56 = (bf16[48,1920]{1,0:T(8,128)(2,1)S(1)}, bf16[48,1920]{1,0:T(8,128)(2,1)S(1)}, u32[]{:S(2)}, u32[]{:S(2)}) collective-permute-start(bf16[48,1920]{1,0:T(8,128)(2,1)S(1)} %get-tuple-element.113.refs_3_), channel_id=1, source_target_pairs={{0,16},{4,20},{8,24},{12,28},{16,0},{20,4},{24,8},{28,12},{1,17},{... | collective-permute-start | bytes 552968 | tf_op jit(solution)/shard_map/ppermute | solution.py:21
  172.2 23.2 %collective-permute-start.48 = (bf16[48,1920]{1,0:T(8,128)(2,1)S(1)}, bf16[48,1920]{1,0:T(8,128)(2,1)S(1)}, u32[]{:S(2)}, u32[]{:S(2)}) collective-permute-start(bf16[48,1920]{1,0:T(8,128)(2,1)S(1)} %get-tuple-element.114.refs_0_), channel_id=1, source_target_pairs={{0,16},{4,20},{8,24},{12,28},{16,0},{20,4},{24,8},{28,12},{1,17},{... | collective-permute-start | bytes 552968 | tf_op jit(solution)/shard_map/ppermute | solution.py:21
  199.9 15.3 %collective-permute-start.51 = (bf16[48,1920]{1,0:T(8,128)(2,1)S(1)}, bf16[48,1920]{1,0:T(8,128)(2,1)S(1)}, u32[]{:S(2)}, u32[]{:S(2)}) collective-permute-start(bf16[48,1920]{1,0:T(8,128)(2,1)S(1)} %collective-permute-done.48.refs_1_), channel_id=1, source_target_pairs={{0,4},{4,0},{8,12},{12,8},{16,20},{20,16},{24,28},{28,24},{1,5},{5... | collective-permute-start | bytes 552968 | tf_op jit(solution)/shard_map/ppermute | solution.py:21
  203.9 14.3 %collective-permute-start.62 = (bf16[48,1920]{1,0:T(8,128)(2,1)S(1)}, bf16[48,1920]{1,0:T(8,128)(2,1)S(1)}, u32[]{:S(2)}, u32[]{:S(2)}) collective-permute-start(bf16[48,1920]{1,0:T(8,128)(2,1)S(1)} %collective-permute-done.57.refs_5_), channel_id=1, source_target_pairs={{0,4},{4,0},{8,12},{12,8},{16,20},{20,16},{24,28},{28,24},{1,5},{5... | collective-permute-start | bytes 552968 | tf_op jit(solution)/shard_map/ppermute | solution.py:21
  205.4 14.8 %collective-permute-start.54 = (bf16[48,1920]{1,0:T(8,128)(2,1)S(1)}, bf16[48,1920]{1,0:T(8,128)(2,1)S(1)}, u32[]{:S(2)}, u32[]{:S(2)}) collective-permute-start(bf16[48,1920]{1,0:T(8,128)(2,1)S(1)} %collective-permute-done.49.refs_0_), channel_id=1, source_target_pairs={{0,4},{4,0},{8,12},{12,8},{16,20},{20,16},{24,28},{28,24},{1,5},{5... | collective-permute-start | bytes 552968 | tf_op jit(solution)/shard_map/ppermute | solution.py:21
  (107 other events, 1151.2 us)
where the time goes:
time: 226 us; the launch traced here: 225 us
  waiting for transfers between devices  83 us (37%)
  starting transfers between devices  72.6 us (32%)
  Pallas kernels  38.8 us (17%)
  local copies, waits for them, and re-layouts  13.7 us (6%)
  other arithmetic  10.1 us (4%)
  matrix products  5.07 us (2%)
    ppermute x72, waiting for transfers between devices, swap(): return lax.ppermute(value, axis, [(i, i ^ offset) for i in range(size)])  83 us
    ppermute x72, starting transfers between devices, swap(): return lax.ppermute(value, axis, [(i, i ^ offset) for i in range(size)])  72.6 us
    pallas_call x5, Pallas kernels, call(): pl.pallas_call(body, out_shape=[jax.ShapeDtypeStruct(shape, dtype) for sh...  31.8 us
    dynamic_slice x11, local copies, waits for them, and re-layouts, columns(): lax.dynamic_slice_in_dim(arr, owner * block + low, block, arr.ndim - 1)  7.52 us
    pallas_call x2, Pallas kernels, rows_in_place(): pl.pallas_call(body, out_shape=[jax.ShapeDtypeStruct((total, width), F32)...  6.98 us
  transfers between devices with their start and end apart: 72, of which 33 were waited for; matrix products, arithmetic and copies ran while one was open for 10% of the time, Pallas kernels for 10%

commit v1 on v0

--- a/solution.py
+++ b/solution.py
@@ -8,6 +8,7 @@
 
 HEADS = 16
 LANES = 128
+ATTEND_ROWS = 512
 F32 = jnp.float32
 BF16 = jnp.bfloat16
 
@@ -74,23 +75,28 @@
 
     def body(index, *refs):
         parts, rest, (mixed, stat) = refs[:groups], refs[groups : 2 * groups], refs[2 * groups :]
-        outs = [[] for _ in parts]
+        outs = []
         for low in range(0, width, head_dim):
             cols = slice(low, low + head_dim)
-            k = jnp.concatenate([part[1, :, cols] for part in parts])
-            v = jnp.concatenate([part[2, :, cols] for part in parts])
-            for m, part in enumerate(parts):
+            q, k, v = [jnp.concatenate([part[i, :, cols] for part in parts]) for i in range(3)]
+            heads = []
+            for first in range(0, length, ATTEND_ROWS):
                 scores = lax.dot_general(
-                    part[0, :, cols], k, (((1,), (1,)), ((), ())), preferred_element_type=F32
+                    q[first : first + ATTEND_ROWS],
+                    k,
+                    (((1,), (1,)), ((), ())),
+                    preferred_element_type=F32,
                 )
                 scores = scores * scale
                 expo = jnp.exp(scores - jnp.max(scores, axis=1, keepdims=True))
                 total = jnp.sum(expo, axis=1, keepdims=True)
                 summed = jnp.dot(expo.astype(BF16), v, preferred_element_type=F32)
-                outs[m].append((summed / total).astype(BF16))
+                heads.append((summed / total).astype(BF16))
+            outs.append(jnp.concatenate(heads))
+        attention = jnp.concatenate(outs, axis=1)
         for m, part in enumerate(rest):
             start = pl.multiple_of((index[0] ^ m) * rows, rows)
-            value = part[0].astype(F32) + jnp.concatenate(outs[m], axis=1).astype(F32)
+            value = part[0].astype(F32) + attention[m * rows : (m + 1) * rows].astype(F32)
             centred, stat[:, pl.ds(start, rows)] = moments(value)
             mixed[pl.ds(start, rows), :] = centred.astype(BF16)
 
@@ -505,7 +511,6 @@
     steps = len(near)
     for item in outs:
         item.split()
-    (sums,) = together(outs, sums)
     for item in outs:
         item.join()
 

time: 226 us -> 223 us (0.987)
  Pallas kernels: 38.8 us -> 36.4 us
    pallas_call x5, Pallas kernels: 31.8 us -> 29.4 us  [call(): pl.pallas_call(body, out_shape=[jax.ShapeDtypeStruct(shape, dtype) for sh...]
  transfers between devices with their start and end apart: 72 -> 72, of which waited for: 33 -> 33; matrix products, arithmetic and copies ran while one was open for 10% -> 10% of each run, Pallas kernels for 10% -> 9%
where the time goes in v1:
time: 223 us
  waiting for transfers between devices  83 us (37%)
  starting transfers between devices  72.6 us (33%)
  Pallas kernels  36.4 us (16%)
  local copies, waits for them, and re-layouts  13.7 us (6%)
  other arithmetic  10.1 us (5%)
  matrix products  5.07 us (2%)
    ppermute x72, waiting for transfers between devices, swap(): return lax.ppermute(value, axis, [(i, i ^ offset) for i in range(size)])  83 us
    ppermute x72, starting transfers between devices, swap(): return lax.ppermute(value, axis, [(i, i ^ offset) for i in range(size)])  72.6 us
    pallas_call x5, Pallas kernels, call(): pl.pallas_call(body, out_shape=[jax.ShapeDtypeStruct(shape, dtype) for sh...  29.4 us
    dynamic_slice x11, local copies, waits for them, and re-layouts, columns(): lax.dynamic_slice_in_dim(arr, owner * block + low, block, arr.ndim - 1)  7.52 us
    pallas_call x2, Pallas kernels, rows_in_place(): pl.pallas_call(body, out_shape=[jax.ShapeDtypeStruct((total, width), F32)...  6.98 us
  transfers between devices with their start and end apart: 72, of which 33 were waited for; matrix products, arithmetic and copies ran while one was open for 10% of the time, Pallas kernels for 9%

profile of v1, /device:TPU:0, one launch (start us, length us, event | category | flops | bytes accessed | tf_op | source)
XLA Modules:
  0.0 222.6 jit_solution(15371392684730947740)
XLA Ops:
  2.6 2.4 %collective-permute-start.5 = (bf16[1,128,384]{2,1,0:T(8,128)(2,1)}, bf16[1,128,384]{2,1,0:T(8,128)(2,1)}, u32[]{:S(2)}, u32[]{:S(2)}) collective-permute-start(bf16[1,128,384]{2,1,0:T(8,128)(2,1)} %get-tuple-element.91), channel_id=1, source_target_pairs={{0,3},{1,2},{2,1},{3,0},{4,7},{5,6},{6,5},{7,4},{8,11},{9,10},{10,... | collective-permute-start | bytes 294920 | tf_op jit(solution)/shard_map/ppermute | solution.py:22
  23.4 8.4 %collective-permute-done.4.refs_6_ = bf16[1,128,384]{2,1,0:T(8,128)(2,1)S(1)} collective-permute-done((bf16[1,128,384]{2,1,0:T(8,128)(2,1)S(1)}, bf16[1,128,384]{2,1,0:T(8,128)(2,1)S(1)}, u32[]{:S(2)}, u32[]{:S(2)}) %collective-permute-start.4) | collective-permute-done | bytes 98336 | tf_op jit(solution)/shard_map/ppermute | solution.py:22
  34.2 5.1 %shard_map.121 = (bf16[512,384]{1,0:T(8,128)(2,1)}, f32[2,512]{1,0:T(2,128)}) custom-call(s32[1]{0:T(128)} %bitcast.1.index, bf16[3,128,384]{2,1,0:T(8,128)(2,1)} %pad_maximum_fusion.4.refs_0_, bf16[3,128,384]{2,1,0:T(8,128)(2,1)} %collective-permute-done.refs_1_, bf16[3,128,384]{2,1,0:T(8,128)(2,1)} %collective-permute-done.1.refs_2_, ...), custom_call_target="tpu_custom_call" | custom-call | tf_op jit(solution)/shard_map/pallas_call | solution.py:60
  41.1 2.7 %collective-permute-start.17 = (bf16[2,48,768]{2,1,0:T(8,128)(2,1)S(1)}, bf16[2,48,768]{2,1,0:T(8,128)(2,1)}, u32[]{:S(2)}, u32[]{:S(2)}) collective-permute-start(bf16[2,48,768]{2,1,0:T(8,128)(2,1)S(1)} %pad_maximum_fusion.9.refs_6_), channel_id=1, source_target_pairs={{0,16},{4,20},{8,24},{12,28},{16,0},{20,4},{24,8},{28,12},{1,17},{... | collective-permute-start | bytes 442376 | tf_op jit(solution)/shard_map/ppermute | solution.py:22
  48.3 2.8 %collective-permute-done.17.refs_10_ = bf16[2,48,768]{2,1,0:T(8,128)(2,1)} collective-permute-done((bf16[2,48,768]{2,1,0:T(8,128)(2,1)S(1)}, bf16[2,48,768]{2,1,0:T(8,128)(2,1)}, u32[]{:S(2)}, u32[]{:S(2)}) %collective-permute-start.17) | collective-permute-done | bytes 147488 | tf_op jit(solution)/shard_map/ppermute | solution.py:22
  65.5 3.2 %collective-permute-done.16.refs_9_ = bf16[2,48,768]{2,1,0:T(8,128)(2,1)S(1)} collective-permute-done((bf16[2,48,768]{2,1,0:T(8,128)(2,1)S(1)}, bf16[2,48,768]{2,1,0:T(8,128)(2,1)S(1)}, u32[]{:S(2)}, u32[]{:S(2)}) %collective-permute-start.16) | collective-permute-done | bytes 147488 | tf_op jit(solution)/shard_map/ppermute | solution.py:22
  71.4 8.4 %shard_map.122 = (bf16[512,1536]{1,0:T(8,128)(2,1)}, f32[512,768]{1,0:T(8,128)}, bf16[512,384]{1,0:T(8,128)(2,1)}, f32[512,384]{1,0:T(8,128)}, f32[2,512]{1,0:T(2,128)}) custom-call(s32[1]{0:T(128)} %bitcast.index, bf16[512,384]{1,0:T(8,128)(2,1)} %get-tuple-element.39.refs_0_, bf16[512,384]{1,0:T(8,128)(2,1)} %copy-done.11, ...), custom_call_target="tpu_custom_call" | custom-call | tf_op jit(solution)/shard_map/pallas_call | solution.py:60
  85.4 4.0 %shard_map.123 = (bf16[384,512]{1,0:T(8,128)(2,1)}, f32[512,384]{1,0:T(8,128)}, f32[512,384]{1,0:T(8,128)}, f32[1,512]{1,0:T(1,128)}, f32[2,512]{1,0:T(2,128)}) custom-call(f32[512,384]{1,0:T(8,128)} %get-tuple-element.43.z_ref, f32[1,384]{1,0:T(1,128)} %dynamic_slice.227.gain_ref, f32[512,384]{1,0:T(8,128)} %fusion.22.ds_ref, ...), custom_call_target="tpu_custom_call" | custom-call | tf_op jit(solution)/shard_map/pallas_call | solution.py:60
  98.4 5.9 %shard_map.124 = (bf16[512,768]{1,0:T(8,128)(2,1)}, bf16[512,384]{1,0:T(8,128)(2,1)}) custom-call(f32[512,384]{1,0:T(8,128)} %get-tuple-element.47.e_ref, f32[512,384]{1,0:T(8,128)} %get-tuple-element.48.zhat_ref, f32[1,512]{1,0:T(1,128)} %get-tuple-element.49.inv_ref, f32[512,768]{1,0:T(8,128)} %get-tuple-element.50.p_ref, ...), custom_call_target="tpu_custom_call" | custom-call | tf_op jit(solution)/shard_map/pallas_call | solution.py:60
  106.4 2.9 %collective-permute-start.34 = (bf16[2,48,768]{2,1,0:T(8,128)(2,1)S(1)}, bf16[2,48,768]{2,1,0:T(8,128)(2,1)}, u32[]{:S(2)}, u32[]{:S(2)}) collective-permute-start(bf16[2,48,768]{2,1,0:T(8,128)(2,1)S(1)} %fusion.9), channel_id=1, source_target_pairs={{0,16},{4,20},{8,24},{12,28},{16,0},{20,4},{24,8},{28,12},{1,17},{... | collective-permute-start | bytes 442376 | tf_op jit(solution)/shard_map/ppermute | solution.py:22
  113.6 6.0 %shard_map.125 = f32[32,384]{1,0:T(8,128)} custom-call(bf16[512,384]{1,0:T(8,128)(2,1)} %get-tuple-element.57.dz_ref, bf16[512,384]{1,0:T(8,128)(2,1)} %get-tuple-element.58.y_ref), custom_call_target="tpu_custom_call" | custom-call | tf_op jit(solution)/shard_map/pallas_call | solution.py:60
  120.6 5.4 %collective-permute-done.32 = bf16[2,2,4,48,384]{4,3,2,1,0:T(8,128)(2,1)} collective-permute-done((bf16[2,2,4,48,384]{4,3,2,1,0:T(8,128)(2,1)S(1)}, bf16[2,2,4,48,384]{4,3,2,1,0:T(8,128)(2,1)}, u32[]{:S(2)}, u32[]{:S(2)}) %collective-permute-start.32) | collective-permute-done | bytes 589856 | tf_op jit(solution)/shard_map/ppermute | solution.py:22
  131.0 2.7 %collective-permute-start.43 = (bf16[2,4,48,384]{3,2,1,0:T(8,128)(2,1)S(1)}, bf16[2,4,48,384]{3,2,1,0:T(8,128)(2,1)S(1)}, u32[]{:S(2)}, u32[]{:S(2)}) collective-permute-start(bf16[2,4,48,384]{3,2,1,0:T(8,128)(2,1)S(1)} %fusion.3), channel_id=1, source_target_pairs={{0,16},{4,20},{8,24},{12,28},{16,0},{20,4},{24,8},{28,12},{1,17},{... | collective-permute-start | bytes 884744 | tf_op jit(solution)/shard_map/ppermute | solution.py:22
  134.9 2.5 %collective-permute-start.64 = (bf16[48,768]{1,0:T(8,128)(2,1)S(1)}, bf16[48,768]{1,0:T(8,128)(2,1)S(1)}, u32[]{:S(2)}, u32[]{:S(2)}) collective-permute-start(bf16[48,768]{1,0:T(8,128)(2,1)S(1)} %fusion.12.refs_6_), channel_id=1, source_target_pairs={{0,16},{4,20},{8,24},{12,28},{16,0},{20,4},{24,8},{28,12},{1,17},{... | collective-permute-start | bytes 221192 | tf_op jit(solution)/shard_map/ppermute | solution.py:22
  137.4 5.5 %collective-permute-done.35 = bf16[2,4,48,384]{3,2,1,0:T(8,128)(2,1)S(1)} collective-permute-done((bf16[2,4,48,384]{3,2,1,0:T(8,128)(2,1)S(1)}, bf16[2,4,48,384]{3,2,1,0:T(8,128)(2,1)S(1)}, u32[]{:S(2)}, u32[]{:S(2)}) %collective-permute-start.35) | collective-permute-done | bytes 294944 | tf_op jit(solution)/shard_map/ppermute | solution.py:22
  145.4 7.4 %collective-permute-done.43 = bf16[2,4,48,384]{3,2,1,0:T(8,128)(2,1)S(1)} collective-permute-done((bf16[2,4,48,384]{3,2,1,0:T(8,128)(2,1)S(1)}, bf16[2,4,48,384]{3,2,1,0:T(8,128)(2,1)S(1)}, u32[]{:S(2)}, u32[]{:S(2)}) %collective-permute-start.43) | collective-permute-done | bytes 294944 | tf_op jit(solution)/shard_map/ppermute | solution.py:22
  173.9 7.9 %collective-permute-done.70.refs_15_ = bf16[48,768]{1,0:T(8,128)(2,1)S(1)} collective-permute-done((bf16[48,768]{1,0:T(8,128)(2,1)S(1)}, bf16[48,768]{1,0:T(8,128)(2,1)S(1)}, u32[]{:S(2)}, u32[]{:S(2)}) %collective-permute-start.70) | collective-permute-done | bytes 73760 | tf_op jit(solution)/shard_map/ppermute | solution.py:22
  181.9 2.7 %collective-permute-start.71 = (f32[32,384]{1,0:T(8,128)S(1)}, f32[32,384]{1,0:T(8,128)S(1)}, u32[]{:S(2)}, u32[]{:S(2)}) collective-permute-start(f32[32,384]{1,0:T(8,128)S(1)} %add.97), channel_id=1, source_target_pairs={{0,16},{4,20},{8,24},{12,28},{16,0},{20,4},{24,8},{28,12},{1,17},{... | collective-permute-start | bytes 147464 | tf_op jit(solution)/shard_map/ppermute | solution.py:22
  184.5 4.5 %collective-permute-done.71 = f32[32,384]{1,0:T(8,128)S(1)} collective-permute-done((f32[32,384]{1,0:T(8,128)S(1)}, f32[32,384]{1,0:T(8,128)S(1)}, u32[]{:S(2)}, u32[]{:S(2)}) %collective-permute-start.71) | collective-permute-done | bytes 49184 | tf_op jit(solution)/shard_map/ppermute | solution.py:22
  193.5 3.0 %collective-permute-done.52.refs_2_ = bf16[48,1920]{1,0:T(8,128)(2,1)S(1)} collective-permute-done((bf16[48,1920]{1,0:T(8,128)(2,1)S(1)}, bf16[48,1920]{1,0:T(8,128)(2,1)S(1)}, u32[]{:S(2)}, u32[]{:S(2)}) %collective-permute-start.52) | collective-permute-done | bytes 184352 | tf_op jit(solution)/shard_map/ppermute | solution.py:22
  204.2 2.9 %shard_map.126 = (f32[384,3072]{1,0:T(8,128)}, f32[384,1536]{1,0:T(8,128)}) custom-call(s32[1]{0:T(128)} %bitcast.index, bf16[48,1920]{1,0:T(8,128)(2,1)} %copy-done.5, bf16[48,1920]{1,0:T(8,128)(2,1)} %copy-done.19, bf16[48,1920]{1,0:T(8,128)(2,1)} %copy-done.20, bf16[48,1920]{1,0:T(8,128)(2,1)} %copy-done.4, bf16[48,1920]{1,0:T(8,128)(2,1)} %copy-done.18, ...), custom_call_target="tpu_custom_call" | custom-call | tf_op jit(solution)/shard_map/pallas_call | solution.py:362
  207.2 5.6 %collective-permute-done.53.refs_3_ = bf16[48,1920]{1,0:T(8,128)(2,1)S(1)} collective-permute-done((bf16[48,1920]{1,0:T(8,128)(2,1)S(1)}, bf16[48,1920]{1,0:T(8,128)(2,1)S(1)}, u32[]{:S(2)}, u32[]{:S(2)}) %collective-permute-start.53) | collective-permute-done | bytes 184352 | tf_op jit(solution)/shard_map/ppermute | solution.py:22
  212.8 3.0 %collective-permute-done.62.refs_9_ = bf16[48,1920]{1,0:T(8,128)(2,1)S(1)} collective-permute-done((bf16[48,1920]{1,0:T(8,128)(2,1)S(1)}, bf16[48,1920]{1,0:T(8,128)(2,1)S(1)}, u32[]{:S(2)}, u32[]{:S(2)}) %collective-permute-start.62) | collective-permute-done | bytes 184352 | tf_op jit(solution)/shard_map/ppermute | solution.py:22
  218.4 4.1 %shard_map.127 = (f32[384,3072]{1,0:T(8,128)}, f32[384,1536]{1,0:T(8,128)}) custom-call(s32[1]{0:T(128)} %bitcast.index, bf16[48,1920]{1,0:T(8,128)(2,1)} %copy-done.25, bf16[48,1920]{1,0:T(8,128)(2,1)} %copy-done.22, bf16[48,1920]{1,0:T(8,128)(2,1)} %copy-done.27, bf16[48,1920]{1,0:T(8,128)(2,1)} %copy-done.28, ...), custom_call_target="tpu_custom_call", output_to_operand_aliasing={{0}: (17, {}), {1}: (18, {})} | custom-call | tf_op jit(solution)/shard_map/pallas_call | solution.py:362
  (318 shorter events, 112.1 us)
Async XLA Ops:
  2.6 14.9 %collective-permute-start.5 = (bf16[1,128,384]{2,1,0:T(8,128)(2,1)}, bf16[1,128,384]{2,1,0:T(8,128)(2,1)}, u32[]{:S(2)}, u32[]{:S(2)}) collective-permute-start(bf16[1,128,384]{2,1,0:T(8,128)(2,1)} %get-tuple-element.91), channel_id=1, source_target_pairs={{0,3},{1,2},{2,1},{3,0},{4,7},{5,6},{6,5},{7,4},{8,11},{9,10},{10,... | collective-permute-start | bytes 294920 | tf_op jit(solution)/shard_map/ppermute | solution.py:22
  7.6 26.2 %collective-permute-start.1 = (bf16[3,128,384]{2,1,0:T(8,128)(2,1)}, bf16[3,128,384]{2,1,0:T(8,128)(2,1)}, u32[]{:S(2)}, u32[]{:S(2)}) collective-permute-start(bf16[3,128,384]{2,1,0:T(8,128)(2,1)} %pad_maximum_fusion.6), channel_id=1, source_target_pairs={{0,2},{1,3},{2,0},{3,1},{4,6},{5,7},{6,4},{7,5},{8,10},{9,11},{10,... | collective-permute-start | bytes 884744 | tf_op jit(solution)/shard_map/ppermute | solution.py:22
  9.8 24.4 %collective-permute-start = (bf16[3,128,384]{2,1,0:T(8,128)(2,1)}, bf16[3,128,384]{2,1,0:T(8,128)(2,1)}, u32[]{:S(2)}, u32[]{:S(2)}) collective-permute-start(bf16[3,128,384]{2,1,0:T(8,128)(2,1)} %pad_maximum_fusion.5), channel_id=1, source_target_pairs={{0,1},{1,0},{2,3},{3,2},{4,5},{5,4},{6,7},{7,6},{8,9},{9,8},{10,11... | collective-permute-start | bytes 884744 | tf_op jit(solution)/shard_map/ppermute | solution.py:22
  10.7 23.5 %collective-permute-start.2 = (bf16[3,128,384]{2,1,0:T(8,128)(2,1)}, bf16[3,128,384]{2,1,0:T(8,128)(2,1)}, u32[]{:S(2)}, u32[]{:S(2)}) collective-permute-start(bf16[3,128,384]{2,1,0:T(8,128)(2,1)} %pad_maximum_fusion.7), channel_id=1, source_target_pairs={{0,3},{1,2},{2,1},{3,0},{4,7},{5,6},{6,5},{7,4},{8,11},{9,10},{10,... | collective-permute-start | bytes 884744 | tf_op jit(solution)/shard_map/ppermute | solution.py:22
  17.4 34.1 %collective-permute-start.9 = (bf16[2,1,128,1536]{3,2,1,0:T(8,128)(2,1)S(1)}, bf16[2,1,128,1536]{3,2,1,0:T(8,128)(2,1)}, u32[]{:S(2)}, u32[]{:S(2)}) collective-permute-start(bf16[2,1,128,1536]{3,2,1,0:T(8,128)(2,1)S(1)} %pad_maximum_fusion.1), channel_id=1, source_target_pairs={{0,1},{1,0},{2,3},{3,2},{4,5},{5,4},{6,7},{7,6},{8,9},{9,8},{10,11... | collective-permute-start | bytes 2359304 | tf_op jit(solution)/shard_map/ppermute | solution.py:22
  53.3 17.1 %collective-permute-start.11 = (bf16[384,768]{1,0:T(8,128)(2,1)S(1)}, bf16[384,768]{1,0:T(8,128)(2,1)S(1)}, u32[]{:S(2)}, u32[]{:S(2)}) collective-permute-start(bf16[384,768]{1,0:T(8,128)(2,1)S(1)} %copy-done.7), channel_id=1, source_target_pairs={{0,1},{1,0},{2,3},{3,2},{4,5},{5,4},{6,7},{7,6},{8,9},{9,8},{10,11... | collective-permute-start | bytes 1769480 | tf_op jit(solution)/shard_map/ppermute | solution.py:22
  54.9 15.6 %collective-permute-start.6 = (bf16[512,384]{1,0:T(8,128)(2,1)S(1)}, bf16[512,384]{1,0:T(8,128)(2,1)S(1)}, u32[]{:S(2)}, u32[]{:S(2)}) collective-permute-start(bf16[512,384]{1,0:T(8,128)(2,1)S(1)} %copy-done.9), channel_id=1, source_target_pairs={{0,1},{1,0},{2,3},{3,2},{4,5},{5,4},{6,7},{7,6},{8,9},{9,8},{10,11... | collective-permute-start | bytes 1179656 | tf_op jit(solution)/shard_map/ppermute | solution.py:22
  91.5 12.9 %collective-permute-start.27 = (bf16[2,2,48,768]{3,2,0,1:T(8,128)(2,1)S(1)}, bf16[2,2,48,768]{3,2,0,1:T(8,128)(2,1)S(1)}, u32[]{:S(2)}, u32[]{:S(2)}) collective-permute-start(bf16[2,2,48,768]{3,2,0,1:T(8,128)(2,1)S(1)} %fusion.4), channel_id=1, source_target_pairs={{0,4},{4,0},{8,12},{12,8},{16,20},{20,16},{24,28},{28,24},{1,5},{5... | collective-permute-start | bytes 884744 | tf_op jit(solution)/shard_map/ppermute | solution.py:22
  105.2 14.3 %collective-permute-start.33 = (bf16[2,48,768]{2,1,0:T(8,128)(2,1)}, bf16[2,48,768]{2,1,0:T(8,128)(2,1)S(1)}, u32[]{:S(2)}, u32[]{:S(2)}) collective-permute-start(bf16[2,48,768]{2,1,0:T(8,128)(2,1)} %fusion.8), channel_id=1, source_target_pairs={{0,8},{4,12},{8,0},{12,4},{16,24},{20,28},{24,16},{28,20},{1,9},{5... | collective-permute-start | bytes 442376 | tf_op jit(solution)/shard_map/ppermute | solution.py:22
  106.4 13.2 %collective-permute-start.34 = (bf16[2,48,768]{2,1,0:T(8,128)(2,1)S(1)}, bf16[2,48,768]{2,1,0:T(8,128)(2,1)}, u32[]{:S(2)}, u32[]{:S(2)}) collective-permute-start(bf16[2,48,768]{2,1,0:T(8,128)(2,1)S(1)} %fusion.9), channel_id=1, source_target_pairs={{0,16},{4,20},{8,24},{12,28},{16,0},{20,4},{24,8},{28,12},{1,17},{... | collective-permute-start | bytes 442376 | tf_op jit(solution)/shard_map/ppermute | solution.py:22
  111.9 14.2 %collective-permute-start.32 = (bf16[2,2,4,48,384]{4,3,2,1,0:T(8,128)(2,1)S(1)}, bf16[2,2,4,48,384]{4,3,2,1,0:T(8,128)(2,1)}, u32[]{:S(2)}, u32[]{:S(2)}) collective-permute-start(bf16[2,2,4,48,384]{4,3,2,1,0:T(8,128)(2,1)S(1)} %fusion), channel_id=1, source_target_pairs={{0,4},{4,0},{8,12},{12,8},{16,20},{20,16},{24,28},{28,24},{1,5},{5... | collective-permute-start | bytes 1769480 | tf_op jit(solution)/shard_map/ppermute | solution.py:22
  112.5 18.3 %collective-permute-start.42 = (bf16[2,2,4,48,384]{4,3,2,1,0:T(8,128)(2,1)S(1)}, bf16[2,2,4,48,384]{4,3,2,1,0:T(8,128)(2,1)S(1)}, u32[]{:S(2)}, u32[]{:S(2)}) collective-permute-start(bf16[2,2,4,48,384]{4,3,2,1,0:T(8,128)(2,1)S(1)} %fusion.1), channel_id=1, source_target_pairs={{0,8},{4,12},{8,0},{12,4},{16,24},{20,28},{24,16},{28,20},{1,9},{5... | collective-permute-start | bytes 1769480 | tf_op jit(solution)/shard_map/ppermute | solution.py:22
  129.8 13.1 %collective-permute-start.35 = (bf16[2,4,48,384]{3,2,1,0:T(8,128)(2,1)S(1)}, bf16[2,4,48,384]{3,2,1,0:T(8,128)(2,1)S(1)}, u32[]{:S(2)}, u32[]{:S(2)}) collective-permute-start(bf16[2,4,48,384]{3,2,1,0:T(8,128)(2,1)S(1)} %fusion.2), channel_id=1, source_target_pairs={{0,8},{4,12},{8,0},{12,4},{16,24},{20,28},{24,16},{28,20},{1,9},{5... | collective-permute-start | bytes 884744 | tf_op jit(solution)/shard_map/ppermute | solution.py:22
  131.0 21.8 %collective-permute-start.43 = (bf16[2,4,48,384]{3,2,1,0:T(8,128)(2,1)S(1)}, bf16[2,4,48,384]{3,2,1,0:T(8,128)(2,1)S(1)}, u32[]{:S(2)}, u32[]{:S(2)}) collective-permute-start(bf16[2,4,48,384]{3,2,1,0:T(8,128)(2,1)S(1)} %fusion.3), channel_id=1, source_target_pairs={{0,16},{4,20},{8,24},{12,28},{16,0},{20,4},{24,8},{28,12},{1,17},{... | collective-permute-start | bytes 884744 | tf_op jit(solution)/shard_map/ppermute | solution.py:22
  133.8 27.3 %collective-permute-start.65 = (bf16[48,768]{1,0:T(8,128)(2,1)S(1)}, bf16[48,768]{1,0:T(8,128)(2,1)S(1)}, u32[]{:S(2)}, u32[]{:S(2)}) collective-permute-start(bf16[48,768]{1,0:T(8,128)(2,1)S(1)} %fusion.12.refs_6_), channel_id=1, source_target_pairs={{0,4},{4,0},{8,12},{12,8},{16,20},{20,16},{24,28},{28,24},{1,5},{5... | collective-permute-start | bytes 221192 | tf_op jit(solution)/shard_map/ppermute | solution.py:22
  134.9 26.3 %collective-permute-start.64 = (bf16[48,768]{1,0:T(8,128)(2,1)S(1)}, bf16[48,768]{1,0:T(8,128)(2,1)S(1)}, u32[]{:S(2)}, u32[]{:S(2)}) collective-permute-start(bf16[48,768]{1,0:T(8,128)(2,1)S(1)} %fusion.12.refs_6_), channel_id=1, source_target_pairs={{0,16},{4,20},{8,24},{12,28},{16,0},{20,4},{24,8},{28,12},{1,17},{... | collective-permute-start | bytes 221192 | tf_op jit(solution)/shard_map/ppermute | solution.py:22
  143.0 12.4 %collective-permute-start.38 = (bf16[4,48,384]{2,1,0:T(8,128)(2,1)S(1)}, bf16[4,48,384]{2,1,0:T(8,128)(2,1)S(1)}, u32[]{:S(2)}, u32[]{:S(2)}) collective-permute-start(bf16[4,48,384]{2,1,0:T(8,128)(2,1)S(1)} %fusion.10), channel_id=1, source_target_pairs={{0,16},{4,20},{8,24},{12,28},{16,0},{20,4},{24,8},{28,12},{1,17},{... | collective-permute-start | bytes 442376 | tf_op jit(solution)/shard_map/ppermute | solution.py:22
  165.6 23.9 %collective-permute-start.60 = (bf16[48,1920]{1,0:T(8,128)(2,1)S(1)}, bf16[48,1920]{1,0:T(8,128)(2,1)S(1)}, u32[]{:S(2)}, u32[]{:S(2)}) collective-permute-start(bf16[48,1920]{1,0:T(8,128)(2,1)S(1)} %get-tuple-element.107.refs_3_), channel_id=1, source_target_pairs={{0,8},{4,12},{8,0},{12,4},{16,24},{20,28},{24,16},{28,20},{1,9},{5... | collective-permute-start | bytes 552968 | tf_op jit(solution)/shard_map/ppermute | solution.py:22
  166.3 23.7 %collective-permute-start.58 = (bf16[48,1920]{1,0:T(8,128)(2,1)S(1)}, bf16[48,1920]{1,0:T(8,128)(2,1)S(1)}, u32[]{:S(2)}, u32[]{:S(2)}) collective-permute-start(bf16[48,1920]{1,0:T(8,128)(2,1)S(1)} %get-tuple-element.107.refs_3_), channel_id=1, source_target_pairs={{0,4},{4,0},{8,12},{12,8},{16,20},{20,16},{24,28},{28,24},{1,5},{5... | collective-permute-start | bytes 552968 | tf_op jit(solution)/shard_map/ppermute | solution.py:22
  168.9 22.6 %collective-permute-start.56 = (bf16[48,1920]{1,0:T(8,128)(2,1)S(1)}, bf16[48,1920]{1,0:T(8,128)(2,1)S(1)}, u32[]{:S(2)}, u32[]{:S(2)}) collective-permute-start(bf16[48,1920]{1,0:T(8,128)(2,1)S(1)} %get-tuple-element.107.refs_3_), channel_id=1, source_target_pairs={{0,16},{4,20},{8,24},{12,28},{16,0},{20,4},{24,8},{28,12},{1,17},{... | collective-permute-start | bytes 552968 | tf_op jit(solution)/shard_map/ppermute | solution.py:22
  169.8 23.3 %collective-permute-start.48 = (bf16[48,1920]{1,0:T(8,128)(2,1)S(1)}, bf16[48,1920]{1,0:T(8,128)(2,1)S(1)}, u32[]{:S(2)}, u32[]{:S(2)}) collective-permute-start(bf16[48,1920]{1,0:T(8,128)(2,1)S(1)} %get-tuple-element.108.refs_0_), channel_id=1, source_target_pairs={{0,16},{4,20},{8,24},{12,28},{16,0},{20,4},{24,8},{28,12},{1,17},{... | collective-permute-start | bytes 552968 | tf_op jit(solution)/shard_map/ppermute | solution.py:22
  197.5 15.3 %collective-permute-start.51 = (bf16[48,1920]{1,0:T(8,128)(2,1)S(1)}, bf16[48,1920]{1,0:T(8,128)(2,1)S(1)}, u32[]{:S(2)}, u32[]{:S(2)}) collective-permute-start(bf16[48,1920]{1,0:T(8,128)(2,1)S(1)} %collective-permute-done.48.refs_1_), channel_id=1, source_target_pairs={{0,4},{4,0},{8,12},{12,8},{16,20},{20,16},{24,28},{28,24},{1,5},{5... | collective-permute-start | bytes 552968 | tf_op jit(solution)/shard_map/ppermute | solution.py:22
  201.5 14.2 %collective-permute-start.62 = (bf16[48,1920]{1,0:T(8,128)(2,1)S(1)}, bf16[48,1920]{1,0:T(8,128)(2,1)S(1)}, u32[]{:S(2)}, u32[]{:S(2)}) collective-permute-start(bf16[48,1920]{1,0:T(8,128)(2,1)S(1)} %collective-permute-done.57.refs_5_), channel_id=1, source_target_pairs={{0,4},{4,0},{8,12},{12,8},{16,20},{20,16},{24,28},{28,24},{1,5},{5... | collective-permute-start | bytes 552968 | tf_op jit(solution)/shard_map/ppermute | solution.py:22
  202.9 14.8 %collective-permute-start.54 = (bf16[48,1920]{1,0:T(8,128)(2,1)S(1)}, bf16[48,1920]{1,0:T(8,128)(2,1)S(1)}, u32[]{:S(2)}, u32[]{:S(2)}) collective-permute-start(bf16[48,1920]{1,0:T(8,128)(2,1)S(1)} %collective-permute-done.49.refs_0_), channel_id=1, source_target_pairs={{0,4},{4,0},{8,12},{12,8},{16,20},{20,16},{24,28},{28,24},{1,5},{5... | collective-permute-start | bytes 552968 | tf_op jit(solution)/shard_map/ppermute | solution.py:22
  (107 other events, 1141.3 us)

commit v2 on v1

--- a/solution.py
+++ b/solution.py
@@ -116,7 +116,7 @@
             padded[i, half + low : half + low + LANES] = read(low, i * tile, tile)
 
 
-def convolve(padded, taps, length, width, places, write, chunk=64):
+def convolve(padded, taps, length, width, places, write, chunk=128):
     tile = tile_width(width)
     for i in range(width // tile):
         cols = slice(i * tile, (i + 1) * tile)
@@ -373,19 +373,17 @@
     )(index_of(axis).astype(jnp.int32).reshape(1), *[job[0] for job in jobs], *into)
 
 
-def gather_both(glu, out, near, far):
-    share, wide = glu.shape
-    width = out.shape[1]
+def gather_both(left, right, out, near, far):
+    share, middle = left.shape
+    wide, width = 2 * middle, out.shape[1]
     cut = width // 2
-    both = jnp.concatenate([glu, out[:, :cut]], axis=1)
-    middle = (wide + cut) // 2
-    if share % 16 == 0 and middle % LANES == 0 and middle <= wide:
-        one = tree(both[:, :middle], "dp", near)
-        two = tree(both[:, middle:], "dp", near)
+    if share % 16 == 0 and cut % LANES == 0:
+        one = tree(left, "dp", near)
+        two = tree(jnp.concatenate([right, out[:, :cut]], axis=1), "dp", near)
         short = tree(out[:, cut:], "dp", far)
         spans = [(0, 0, middle, 0)], [
             (0, 0, wide - middle, middle),
-            (1, wide - middle, middle, 0),
+            (1, middle, middle + cut, 0),
         ]
         jobs = [(part, o, spans[i]) for i, parts in enumerate((one, two)) for o, part in parts.items()]
         jobs += [(part, o, [(1, 0, cut, cut)]) for o, part in short.items()]
@@ -395,10 +393,9 @@
         rest = [job for job in jobs if not any(job is other for other in early)]
         into = rows_in_place(early, (wide, width), "dp")
         return rows_in_place(rest, (wide, width), "dp", into)
-    long, short = both, out[:, cut:]
-    long = gather_rows(long, "dp", near).reshape(-1, wide + cut).astype(F32)
-    short = gather_rows(short, "dp", far).reshape(-1, width - cut).astype(F32)
-    return long[:, :wide], jnp.concatenate([long[:, wide:], short], axis=1)
+    glu = gather_rows(jnp.concatenate([left, right], axis=1), "dp", near).reshape(-1, wide)
+    out = gather_rows(out, "dp", far).reshape(-1, width)
+    return glu.astype(F32), out.astype(F32)
 
 
 class Halving:
@@ -550,15 +547,16 @@
     for item in glus:
         part = item.value.astype(BF16)
         got = jnp.stack([part[0]] + [swap(part[o], "tm", o) for o in offsets[1:]])
+        if pieces:
+            got, _ = lax.optimization_barrier((got, pieces[0]))
         ordered = [
             lax.dynamic_index_in_dim(got, mine ^ g, 0, keepdims=False) for g in range(groups)
         ]
-        pieces += ordered
+        pieces.append(jnp.concatenate(ordered, axis=1))
     out_piece = jnp.concatenate([item.value.astype(BF16) for item in outs], axis=1)
-    glu_piece = jnp.concatenate(pieces, axis=1)
-    (taps_sum, glu_piece) = lax.optimization_barrier((taps_sum, glu_piece))
+    (taps_sum, pieces[1]) = lax.optimization_barrier((taps_sum, pieces[1]))
     taps_sum = taps_sum + swap(taps_sum, "dp", near[-1])
-    glu_grad, out_grad = gather_both(glu_piece, out_piece, near[::-1], far[::-1])
+    glu_grad, out_grad = gather_both(*pieces, out_piece, near[::-1], far[::-1])
     return (glu_grad, taps_sum, out_grad)
 
 

time: 223 us -> 221 us (level)
  waiting for transfers between devices: 83 us -> 76.7 us
  starting transfers between devices: 72.6 us -> 76.6 us
    ppermute x72, waiting for transfers between devices: 83 us -> 76.7 us  [swap(): return lax.ppermute(value, axis, [(i, i ^ offset) for i in range(size)])]
    ppermute x72, starting transfers between devices: 72.6 us -> 76.6 us  [swap(): return lax.ppermute(value, axis, [(i, i ^ offset) for i in range(size)])]
  transfers between devices with their start and end apart: 72 -> 72, of which waited for: 33 -> 30; matrix products, arithmetic and copies ran while one was open for 10% -> 10% of each run, Pallas kernels for 9% -> 9%
where the time goes in v2:
time: 221 us; the launch traced here: 220 us
  waiting for transfers between devices  76.7 us (35%)
  starting transfers between devices  76.6 us (35%)
  Pallas kernels  36.3 us (16%)
  local copies, waits for them, and re-layouts  13.7 us (6%)
  other arithmetic  10.2 us (5%)
  matrix products  5.07 us (2%)
    ppermute x72, waiting for transfers between devices, swap(): return lax.ppermute(value, axis, [(i, i ^ offset) for i in range(size)])  76.7 us
    ppermute x72, starting transfers between devices, swap(): return lax.ppermute(value, axis, [(i, i ^ offset) for i in range(size)])  76.6 us
    pallas_call x5, Pallas kernels, call(): pl.pallas_call(body, out_shape=[jax.ShapeDtypeStruct(shape, dtype) for sh...  29.3 us
    dynamic_slice x11, local copies, waits for them, and re-layouts, columns(): lax.dynamic_slice_in_dim(arr, owner * block + low, block, arr.ndim - 1)  7.59 us
    pallas_call x2, Pallas kernels, rows_in_place(): pl.pallas_call(body, out_shape=[jax.ShapeDtypeStruct((total, width), F32)...  7.01 us
  transfers between devices with their start and end apart: 72, of which 30 were waited for; matrix products, arithmetic and copies ran while one was open for 10% of the time, Pallas kernels for 9%

profile of v2, /device:TPU:0, one launch (start us, length us, event | category | flops | bytes accessed | tf_op | source)
XLA Modules:
  0.0 220.4 jit_solution(18008147954181784397)
XLA Ops:
  2.7 2.4 %collective-permute-start.5 = (bf16[1,128,384]{2,1,0:T(8,128)(2,1)}, bf16[1,128,384]{2,1,0:T(8,128)(2,1)}, u32[]{:S(2)}, u32[]{:S(2)}) collective-permute-start(bf16[1,128,384]{2,1,0:T(8,128)(2,1)} %get-tuple-element.93), channel_id=1, source_target_pairs={{0,3},{1,2},{2,1},{3,0},{4,7},{5,6},{6,5},{7,4},{8,11},{9,10},{10,... | collective-permute-start | bytes 294920 | tf_op jit(solution)/shard_map/ppermute | solution.py:22
  23.5 8.4 %collective-permute-done.4.refs_6_ = bf16[1,128,384]{2,1,0:T(8,128)(2,1)S(1)} collective-permute-done((bf16[1,128,384]{2,1,0:T(8,128)(2,1)S(1)}, bf16[1,128,384]{2,1,0:T(8,128)(2,1)S(1)}, u32[]{:S(2)}, u32[]{:S(2)}) %collective-permute-start.4) | collective-permute-done | bytes 98336 | tf_op jit(solution)/shard_map/ppermute | solution.py:22
  34.2 5.1 %shard_map.121 = (bf16[512,384]{1,0:T(8,128)(2,1)}, f32[2,512]{1,0:T(2,128)}) custom-call(s32[1]{0:T(128)} %bitcast.1.index, bf16[3,128,384]{2,1,0:T(8,128)(2,1)} %pad_maximum_fusion.4.refs_0_, bf16[3,128,384]{2,1,0:T(8,128)(2,1)} %collective-permute-done.refs_1_, bf16[3,128,384]{2,1,0:T(8,128)(2,1)} %collective-permute-done.1.refs_2_, ...), custom_call_target="tpu_custom_call" | custom-call | tf_op jit(solution)/shard_map/pallas_call | solution.py:60
  41.1 2.7 %collective-permute-start.17 = (bf16[2,48,768]{2,1,0:T(8,128)(2,1)S(1)}, bf16[2,48,768]{2,1,0:T(8,128)(2,1)}, u32[]{:S(2)}, u32[]{:S(2)}) collective-permute-start(bf16[2,48,768]{2,1,0:T(8,128)(2,1)S(1)} %pad_maximum_fusion.9.refs_6_), channel_id=1, source_target_pairs={{0,16},{4,20},{8,24},{12,28},{16,0},{20,4},{24,8},{28,12},{1,17},{... | collective-permute-start | bytes 442376 | tf_op jit(solution)/shard_map/ppermute | solution.py:22
  48.3 2.8 %collective-permute-done.17.refs_10_ = bf16[2,48,768]{2,1,0:T(8,128)(2,1)} collective-permute-done((bf16[2,48,768]{2,1,0:T(8,128)(2,1)S(1)}, bf16[2,48,768]{2,1,0:T(8,128)(2,1)}, u32[]{:S(2)}, u32[]{:S(2)}) %collective-permute-start.17) | collective-permute-done | bytes 147488 | tf_op jit(solution)/shard_map/ppermute | solution.py:22
  65.5 3.2 %collective-permute-done.16.refs_9_ = bf16[2,48,768]{2,1,0:T(8,128)(2,1)S(1)} collective-permute-done((bf16[2,48,768]{2,1,0:T(8,128)(2,1)S(1)}, bf16[2,48,768]{2,1,0:T(8,128)(2,1)S(1)}, u32[]{:S(2)}, u32[]{:S(2)}) %collective-permute-start.16) | collective-permute-done | bytes 147488 | tf_op jit(solution)/shard_map/ppermute | solution.py:22
  71.5 8.1 %shard_map.122 = (bf16[512,1536]{1,0:T(8,128)(2,1)}, f32[512,768]{1,0:T(8,128)}, bf16[512,384]{1,0:T(8,128)(2,1)}, f32[512,384]{1,0:T(8,128)}, f32[2,512]{1,0:T(2,128)}) custom-call(s32[1]{0:T(128)} %bitcast.index, bf16[512,384]{1,0:T(8,128)(2,1)} %get-tuple-element.40.refs_0_, bf16[512,384]{1,0:T(8,128)(2,1)} %copy-done.11, ...), custom_call_target="tpu_custom_call" | custom-call | tf_op jit(solution)/shard_map/pallas_call | solution.py:60
  85.1 4.0 %shard_map.123 = (bf16[384,512]{1,0:T(8,128)(2,1)}, f32[512,384]{1,0:T(8,128)}, f32[512,384]{1,0:T(8,128)}, f32[1,512]{1,0:T(1,128)}, f32[2,512]{1,0:T(2,128)}) custom-call(f32[512,384]{1,0:T(8,128)} %get-tuple-element.44.z_ref, f32[1,384]{1,0:T(1,128)} %dynamic_slice.227.gain_ref, f32[512,384]{1,0:T(8,128)} %fusion.22.ds_ref, ...), custom_call_target="tpu_custom_call" | custom-call | tf_op jit(solution)/shard_map/pallas_call | solution.py:60
  98.2 5.9 %shard_map.124 = (bf16[512,768]{1,0:T(8,128)(2,1)}, bf16[512,384]{1,0:T(8,128)(2,1)}) custom-call(f32[512,384]{1,0:T(8,128)} %get-tuple-element.48.e_ref, f32[512,384]{1,0:T(8,128)} %get-tuple-element.49.zhat_ref, f32[1,512]{1,0:T(1,128)} %get-tuple-element.50.inv_ref, f32[512,768]{1,0:T(8,128)} %get-tuple-element.51.p_ref, ...), custom_call_target="tpu_custom_call" | custom-call | tf_op jit(solution)/shard_map/pallas_call | solution.py:60
  106.1 3.0 %collective-permute-start.34 = (bf16[2,48,768]{2,1,0:T(8,128)(2,1)S(1)}, bf16[2,48,768]{2,1,0:T(8,128)(2,1)}, u32[]{:S(2)}, u32[]{:S(2)}) collective-permute-start(bf16[2,48,768]{2,1,0:T(8,128)(2,1)S(1)} %fusion.9), channel_id=1, source_target_pairs={{0,16},{4,20},{8,24},{12,28},{16,0},{20,4},{24,8},{28,12},{1,17},{... | collective-permute-start | bytes 442376 | tf_op jit(solution)/shard_map/ppermute | solution.py:22
  113.3 6.2 %shard_map.125 = f32[32,384]{1,0:T(8,128)} custom-call(bf16[512,384]{1,0:T(8,128)(2,1)} %get-tuple-element.58.dz_ref, bf16[512,384]{1,0:T(8,128)(2,1)} %get-tuple-element.59.y_ref), custom_call_target="tpu_custom_call" | custom-call | tf_op jit(solution)/shard_map/pallas_call | solution.py:60
  120.5 5.2 %collective-permute-done.32 = bf16[2,2,4,48,384]{4,3,2,1,0:T(8,128)(2,1)} collective-permute-done((bf16[2,2,4,48,384]{4,3,2,1,0:T(8,128)(2,1)S(1)}, bf16[2,2,4,48,384]{4,3,2,1,0:T(8,128)(2,1)}, u32[]{:S(2)}, u32[]{:S(2)}) %collective-permute-start.32) | collective-permute-done | bytes 589856 | tf_op jit(solution)/shard_map/ppermute | solution.py:22
  130.7 2.7 %collective-permute-start.50 = (bf16[2,4,48,384]{3,2,1,0:T(8,128)(2,1)S(1)}, bf16[2,4,48,384]{3,2,1,0:T(8,128)(2,1)S(1)}, u32[]{:S(2)}, u32[]{:S(2)}) collective-permute-start(bf16[2,4,48,384]{3,2,1,0:T(8,128)(2,1)S(1)} %fusion.3), channel_id=1, source_target_pairs={{0,16},{4,20},{8,24},{12,28},{16,0},{20,4},{24,8},{28,12},{1,17},{... | collective-permute-start | bytes 884744 | tf_op jit(solution)/shard_map/ppermute | solution.py:22
  134.6 7.9 %collective-permute-done.35 = bf16[2,4,48,384]{3,2,1,0:T(8,128)(2,1)S(1)} collective-permute-done((bf16[2,4,48,384]{3,2,1,0:T(8,128)(2,1)S(1)}, bf16[2,4,48,384]{3,2,1,0:T(8,128)(2,1)S(1)}, u32[]{:S(2)}, u32[]{:S(2)}) %collective-permute-start.35) | collective-permute-done | bytes 294944 | tf_op jit(solution)/shard_map/ppermute | solution.py:22
  142.7 2.9 %collective-permute-start.37 = (bf16[4,48,384]{2,1,0:T(8,128)(2,1)S(1)}, bf16[4,48,384]{2,1,0:T(8,128)(2,1)S(1)}, u32[]{:S(2)}, u32[]{:S(2)}) collective-permute-start(bf16[4,48,384]{2,1,0:T(8,128)(2,1)S(1)} %fusion.10), channel_id=1, source_target_pairs={{0,16},{4,20},{8,24},{12,28},{16,0},{20,4},{24,8},{28,12},{1,17},{... | collective-permute-start | bytes 442376 | tf_op jit(solution)/shard_map/ppermute | solution.py:22
  145.6 2.6 %collective-permute-done.50 = bf16[2,4,48,384]{3,2,1,0:T(8,128)(2,1)S(1)} collective-permute-done((bf16[2,4,48,384]{3,2,1,0:T(8,128)(2,1)S(1)}, bf16[2,4,48,384]{3,2,1,0:T(8,128)(2,1)S(1)}, u32[]{:S(2)}, u32[]{:S(2)}) %collective-permute-start.50) | collective-permute-done | bytes 294944 | tf_op jit(solution)/shard_map/ppermute | solution.py:22
  148.8 3.2 %collective-permute-done.37 = bf16[4,48,384]{2,1,0:T(8,128)(2,1)S(1)} collective-permute-done((bf16[4,48,384]{2,1,0:T(8,128)(2,1)S(1)}, bf16[4,48,384]{2,1,0:T(8,128)(2,1)S(1)}, u32[]{:S(2)}, u32[]{:S(2)}) %collective-permute-start.37) | collective-permute-done | bytes 147488 | tf_op jit(solution)/shard_map/ppermute | solution.py:22
  167.1 2.5 %collective-permute-start.68 = (bf16[48,768]{1,0:T(8,128)(2,1)S(1)}, bf16[48,768]{1,0:T(8,128)(2,1)S(1)}, u32[]{:S(2)}, u32[]{:S(2)}) collective-permute-start(bf16[48,768]{1,0:T(8,128)(2,1)S(1)} %collective-permute-done.65.refs_7_), channel_id=1, source_target_pairs={{0,8},{4,12},{8,0},{12,4},{16,24},{20,28},{24,16},{28,20},{1,9},{5... | collective-permute-start | bytes 221192 | tf_op jit(solution)/shard_map/ppermute | solution.py:22
  169.5 5.9 %collective-permute-done.64.refs_10_ = bf16[48,768]{1,0:T(8,128)(2,1)S(1)} collective-permute-done((bf16[48,768]{1,0:T(8,128)(2,1)S(1)}, bf16[48,768]{1,0:T(8,128)(2,1)S(1)}, u32[]{:S(2)}, u32[]{:S(2)}) %collective-permute-start.64) | collective-permute-done | bytes 73760 | tf_op jit(solution)/shard_map/ppermute | solution.py:22
  184.3 3.4 %collective-permute-start.58 = (bf16[48,2304]{1,0:T(8,128)(2,1)S(1)}, bf16[48,2304]{1,0:T(8,128)(2,1)S(1)}, u32[]{:S(2)}, u32[]{:S(2)}) collective-permute-start(bf16[48,2304]{1,0:T(8,128)(2,1)S(1)} %pad_maximum_fusion.8.refs_3_), channel_id=1, source_target_pairs={{0,4},{4,0},{8,12},{12,8},{16,20},{20,16},{24,28},{28,24},{1,5},{5... | collective-permute-start | bytes 663560 | tf_op jit(solution)/shard_map/ppermute | solution.py:22
  190.3 3.5 %collective-permute-done.60.refs_5_ = bf16[48,2304]{1,0:T(8,128)(2,1)S(1)} collective-permute-done((bf16[48,2304]{1,0:T(8,128)(2,1)S(1)}, bf16[48,2304]{1,0:T(8,128)(2,1)S(1)}, u32[]{:S(2)}, u32[]{:S(2)}) %collective-permute-start.60) | collective-permute-done | bytes 221216 | tf_op jit(solution)/shard_map/ppermute | solution.py:22
  201.8 2.9 %shard_map.126 = (f32[384,3072]{1,0:T(8,128)}, f32[384,1536]{1,0:T(8,128)}) custom-call(s32[1]{0:T(128)} %bitcast.index, bf16[48,1536]{1,0:T(8,128)(2,1)} %copy-done.5, bf16[48,1536]{1,0:T(8,128)(2,1)} %copy-done.27, bf16[48,1536]{1,0:T(8,128)(2,1)} %copy-done.24, bf16[48,2304]{1,0:T(8,128)(2,1)} %copy-done.3, bf16[48,2304]{1,0:T(8,128)(2,1)} %copy-done.16, ...), custom_call_target="tpu_custom_call" | custom-call | tf_op jit(solution)/shard_map/pallas_call | solution.py:362
  204.7 9.0 %collective-permute-done.44.refs_2_ = bf16[48,1536]{1,0:T(8,128)(2,1)S(1)} collective-permute-done((bf16[48,1536]{1,0:T(8,128)(2,1)S(1)}, bf16[48,1536]{1,0:T(8,128)(2,1)S(1)}, u32[]{:S(2)}, u32[]{:S(2)}) %collective-permute-start.44) | collective-permute-done | bytes 147488 | tf_op jit(solution)/shard_map/ppermute | solution.py:22
  216.1 4.1 %shard_map.127 = (f32[384,3072]{1,0:T(8,128)}, f32[384,1536]{1,0:T(8,128)}) custom-call(s32[1]{0:T(128)} %bitcast.index, bf16[48,1536]{1,0:T(8,128)(2,1)} %copy-done.34, bf16[48,1536]{1,0:T(8,128)(2,1)} %copy-done.32, bf16[48,1536]{1,0:T(8,128)(2,1)} %copy-done.35, bf16[48,1536]{1,0:T(8,128)(2,1)} %copy-done.33, ...), custom_call_target="tpu_custom_call", output_to_operand_aliasing={{0}: (17, {}), {1}: (18, {})} | custom-call | tf_op jit(solution)/shard_map/pallas_call | solution.py:362
  (314 shorter events, 111.3 us)
Async XLA Ops:
  2.7 14.9 %collective-permute-start.5 = (bf16[1,128,384]{2,1,0:T(8,128)(2,1)}, bf16[1,128,384]{2,1,0:T(8,128)(2,1)}, u32[]{:S(2)}, u32[]{:S(2)}) collective-permute-start(bf16[1,128,384]{2,1,0:T(8,128)(2,1)} %get-tuple-element.93), channel_id=1, source_target_pairs={{0,3},{1,2},{2,1},{3,0},{4,7},{5,6},{6,5},{7,4},{8,11},{9,10},{10,... | collective-permute-start | bytes 294920 | tf_op jit(solution)/shard_map/ppermute | solution.py:22
  7.6 26.2 %collective-permute-start.1 = (bf16[3,128,384]{2,1,0:T(8,128)(2,1)}, bf16[3,128,384]{2,1,0:T(8,128)(2,1)}, u32[]{:S(2)}, u32[]{:S(2)}) collective-permute-start(bf16[3,128,384]{2,1,0:T(8,128)(2,1)} %pad_maximum_fusion.6), channel_id=1, source_target_pairs={{0,2},{1,3},{2,0},{3,1},{4,6},{5,7},{6,4},{7,5},{8,10},{9,11},{10,... | collective-permute-start | bytes 884744 | tf_op jit(solution)/shard_map/ppermute | solution.py:22
  9.8 24.4 %collective-permute-start = (bf16[3,128,384]{2,1,0:T(8,128)(2,1)}, bf16[3,128,384]{2,1,0:T(8,128)(2,1)}, u32[]{:S(2)}, u32[]{:S(2)}) collective-permute-start(bf16[3,128,384]{2,1,0:T(8,128)(2,1)} %pad_maximum_fusion.5), channel_id=1, source_target_pairs={{0,1},{1,0},{2,3},{3,2},{4,5},{5,4},{6,7},{7,6},{8,9},{9,8},{10,11... | collective-permute-start | bytes 884744 | tf_op jit(solution)/shard_map/ppermute | solution.py:22
  10.7 23.5 %collective-permute-start.2 = (bf16[3,128,384]{2,1,0:T(8,128)(2,1)}, bf16[3,128,384]{2,1,0:T(8,128)(2,1)}, u32[]{:S(2)}, u32[]{:S(2)}) collective-permute-start(bf16[3,128,384]{2,1,0:T(8,128)(2,1)} %pad_maximum_fusion.7), channel_id=1, source_target_pairs={{0,3},{1,2},{2,1},{3,0},{4,7},{5,6},{6,5},{7,4},{8,11},{9,10},{10,... | collective-permute-start | bytes 884744 | tf_op jit(solution)/shard_map/ppermute | solution.py:22
  17.5 34.1 %collective-permute-start.9 = (bf16[2,1,128,1536]{3,2,1,0:T(8,128)(2,1)S(1)}, bf16[2,1,128,1536]{3,2,1,0:T(8,128)(2,1)}, u32[]{:S(2)}, u32[]{:S(2)}) collective-permute-start(bf16[2,1,128,1536]{3,2,1,0:T(8,128)(2,1)S(1)} %pad_maximum_fusion.1), channel_id=1, source_target_pairs={{0,1},{1,0},{2,3},{3,2},{4,5},{5,4},{6,7},{7,6},{8,9},{9,8},{10,11... | collective-permute-start | bytes 2359304 | tf_op jit(solution)/shard_map/ppermute | solution.py:22
  53.3 17.1 %collective-permute-start.11 = (bf16[384,768]{1,0:T(8,128)(2,1)S(1)}, bf16[384,768]{1,0:T(8,128)(2,1)S(1)}, u32[]{:S(2)}, u32[]{:S(2)}) collective-permute-start(bf16[384,768]{1,0:T(8,128)(2,1)S(1)} %copy-done.7), channel_id=1, source_target_pairs={{0,1},{1,0},{2,3},{3,2},{4,5},{5,4},{6,7},{7,6},{8,9},{9,8},{10,11... | collective-permute-start | bytes 1769480 | tf_op jit(solution)/shard_map/ppermute | solution.py:22
  54.9 15.6 %collective-permute-start.6 = (bf16[512,384]{1,0:T(8,128)(2,1)S(1)}, bf16[512,384]{1,0:T(8,128)(2,1)S(1)}, u32[]{:S(2)}, u32[]{:S(2)}) collective-permute-start(bf16[512,384]{1,0:T(8,128)(2,1)S(1)} %copy-done.9), channel_id=1, source_target_pairs={{0,1},{1,0},{2,3},{3,2},{4,5},{5,4},{6,7},{7,6},{8,9},{9,8},{10,11... | collective-permute-start | bytes 1179656 | tf_op jit(solution)/shard_map/ppermute | solution.py:22
  91.2 12.8 %collective-permute-start.27 = (bf16[2,2,48,768]{3,2,0,1:T(8,128)(2,1)S(1)}, bf16[2,2,48,768]{3,2,0,1:T(8,128)(2,1)S(1)}, u32[]{:S(2)}, u32[]{:S(2)}) collective-permute-start(bf16[2,2,48,768]{3,2,0,1:T(8,128)(2,1)S(1)} %fusion.4), channel_id=1, source_target_pairs={{0,4},{4,0},{8,12},{12,8},{16,20},{20,16},{24,28},{28,24},{1,5},{5... | collective-permute-start | bytes 884744 | tf_op jit(solution)/shard_map/ppermute | solution.py:22
  104.9 14.6 %collective-permute-start.33 = (bf16[2,48,768]{2,1,0:T(8,128)(2,1)}, bf16[2,48,768]{2,1,0:T(8,128)(2,1)S(1)}, u32[]{:S(2)}, u32[]{:S(2)}) collective-permute-start(bf16[2,48,768]{2,1,0:T(8,128)(2,1)} %fusion.8), channel_id=1, source_target_pairs={{0,8},{4,12},{8,0},{12,4},{16,24},{20,28},{24,16},{28,20},{1,9},{5... | collective-permute-start | bytes 442376 | tf_op jit(solution)/shard_map/ppermute | solution.py:22
  106.1 13.4 %collective-permute-start.34 = (bf16[2,48,768]{2,1,0:T(8,128)(2,1)S(1)}, bf16[2,48,768]{2,1,0:T(8,128)(2,1)}, u32[]{:S(2)}, u32[]{:S(2)}) collective-permute-start(bf16[2,48,768]{2,1,0:T(8,128)(2,1)S(1)} %fusion.9), channel_id=1, source_target_pairs={{0,16},{4,20},{8,24},{12,28},{16,0},{20,4},{24,8},{28,12},{1,17},{... | collective-permute-start | bytes 442376 | tf_op jit(solution)/shard_map/ppermute | solution.py:22
  111.6 14.2 %collective-permute-start.32 = (bf16[2,2,4,48,384]{4,3,2,1,0:T(8,128)(2,1)S(1)}, bf16[2,2,4,48,384]{4,3,2,1,0:T(8,128)(2,1)}, u32[]{:S(2)}, u32[]{:S(2)}) collective-permute-start(bf16[2,2,4,48,384]{4,3,2,1,0:T(8,128)(2,1)S(1)} %fusion), channel_id=1, source_target_pairs={{0,4},{4,0},{8,12},{12,8},{16,20},{20,16},{24,28},{28,24},{1,5},{5... | collective-permute-start | bytes 1769480 | tf_op jit(solution)/shard_map/ppermute | solution.py:22
  112.2 18.3 %collective-permute-start.49 = (bf16[2,2,4,48,384]{4,3,2,1,0:T(8,128)(2,1)S(1)}, bf16[2,2,4,48,384]{4,3,2,1,0:T(8,128)(2,1)S(1)}, u32[]{:S(2)}, u32[]{:S(2)}) collective-permute-start(bf16[2,2,4,48,384]{4,3,2,1,0:T(8,128)(2,1)S(1)} %fusion.1), channel_id=1, source_target_pairs={{0,8},{4,12},{8,0},{12,4},{16,24},{20,28},{24,16},{28,20},{1,9},{5... | collective-permute-start | bytes 1769480 | tf_op jit(solution)/shard_map/ppermute | solution.py:22
  129.5 13.0 %collective-permute-start.35 = (bf16[2,4,48,384]{3,2,1,0:T(8,128)(2,1)S(1)}, bf16[2,4,48,384]{3,2,1,0:T(8,128)(2,1)S(1)}, u32[]{:S(2)}, u32[]{:S(2)}) collective-permute-start(bf16[2,4,48,384]{3,2,1,0:T(8,128)(2,1)S(1)} %fusion.2), channel_id=1, source_target_pairs={{0,8},{4,12},{8,0},{12,4},{16,24},{20,28},{24,16},{28,20},{1,9},{5... | collective-permute-start | bytes 884744 | tf_op jit(solution)/shard_map/ppermute | solution.py:22
  130.7 17.5 %collective-permute-start.50 = (bf16[2,4,48,384]{3,2,1,0:T(8,128)(2,1)S(1)}, bf16[2,4,48,384]{3,2,1,0:T(8,128)(2,1)S(1)}, u32[]{:S(2)}, u32[]{:S(2)}) collective-permute-start(bf16[2,4,48,384]{3,2,1,0:T(8,128)(2,1)S(1)} %fusion.3), channel_id=1, source_target_pairs={{0,16},{4,20},{8,24},{12,28},{16,0},{20,4},{24,8},{28,12},{1,17},{... | collective-permute-start | bytes 884744 | tf_op jit(solution)/shard_map/ppermute | solution.py:22
  133.4 29.1 %collective-permute-start.65 = (bf16[48,768]{1,0:T(8,128)(2,1)S(1)}, bf16[48,768]{1,0:T(8,128)(2,1)S(1)}, u32[]{:S(2)}, u32[]{:S(2)}) collective-permute-start(bf16[48,768]{1,0:T(8,128)(2,1)S(1)} %fusion.12.refs_6_), channel_id=1, source_target_pairs={{0,4},{4,0},{8,12},{12,8},{16,20},{20,16},{24,28},{28,24},{1,5},{5... | collective-permute-start | bytes 221192 | tf_op jit(solution)/shard_map/ppermute | solution.py:22
  159.5 28.1 %collective-permute-start.56 = (bf16[48,2304]{1,0:T(8,128)(2,1)S(1)}, bf16[48,2304]{1,0:T(8,128)(2,1)S(1)}, u32[]{:S(2)}, u32[]{:S(2)}) collective-permute-start(bf16[48,2304]{1,0:T(8,128)(2,1)S(1)} %pad_maximum_fusion.8.refs_3_), channel_id=1, source_target_pairs={{0,16},{4,20},{8,24},{12,28},{16,0},{20,4},{24,8},{28,12},{1,17},{... | collective-permute-start | bytes 663560 | tf_op jit(solution)/shard_map/ppermute | solution.py:22
  161.7 13.7 %collective-permute-start.64 = (bf16[48,768]{1,0:T(8,128)(2,1)S(1)}, bf16[48,768]{1,0:T(8,128)(2,1)S(1)}, u32[]{:S(2)}, u32[]{:S(2)}) collective-permute-start(bf16[48,768]{1,0:T(8,128)(2,1)S(1)} %fusion.12.refs_6_), channel_id=1, source_target_pairs={{0,16},{4,20},{8,24},{12,28},{16,0},{20,4},{24,8},{28,12},{1,17},{... | collective-permute-start | bytes 221192 | tf_op jit(solution)/shard_map/ppermute | solution.py:22
  162.5 14.3 %collective-permute-start.66 = (bf16[48,768]{1,0:T(8,128)(2,1)S(1)}, bf16[48,768]{1,0:T(8,128)(2,1)S(1)}, u32[]{:S(2)}, u32[]{:S(2)}) collective-permute-start(bf16[48,768]{1,0:T(8,128)(2,1)S(1)} %collective-permute-done.65.refs_7_), channel_id=1, source_target_pairs={{0,16},{4,20},{8,24},{12,28},{16,0},{20,4},{24,8},{28,12},{1,17},{... | collective-permute-start | bytes 221192 | tf_op jit(solution)/shard_map/ppermute | solution.py:22
  164.6 19.6 %collective-permute-start.45 = (bf16[48,1536]{1,0:T(8,128)(2,1)S(1)}, bf16[48,1536]{1,0:T(8,128)(2,1)S(1)}, u32[]{:S(2)}, u32[]{:S(2)}) collective-permute-start(bf16[48,1536]{1,0:T(8,128)(2,1)S(1)} %pad_maximum_fusion.11.refs_0_), channel_id=1, source_target_pairs={{0,8},{4,12},{8,0},{12,4},{16,24},{20,28},{24,16},{28,20},{1,9},{5... | collective-permute-start | bytes 442376 | tf_op jit(solution)/shard_map/ppermute | solution.py:22
  193.8 20.0 %collective-permute-start.61 = (bf16[48,2304]{1,0:T(8,128)(2,1)S(1)}, bf16[48,2304]{1,0:T(8,128)(2,1)S(1)}, u32[]{:S(2)}, u32[]{:S(2)}) collective-permute-start(bf16[48,2304]{1,0:T(8,128)(2,1)S(1)} %collective-permute-done.60.refs_5_), channel_id=1, source_target_pairs={{0,4},{4,0},{8,12},{12,8},{16,20},{20,16},{24,28},{28,24},{1,5},{5... | collective-permute-start | bytes 663560 | tf_op jit(solution)/shard_map/ppermute | solution.py:22
  196.2 17.6 %collective-permute-start.59 = (bf16[48,2304]{1,0:T(8,128)(2,1)S(1)}, bf16[48,2304]{1,0:T(8,128)(2,1)S(1)}, u32[]{:S(2)}, u32[]{:S(2)}) collective-permute-start(bf16[48,2304]{1,0:T(8,128)(2,1)S(1)} %collective-permute-done.56.refs_4_), channel_id=1, source_target_pairs={{0,4},{4,0},{8,12},{12,8},{16,20},{20,16},{24,28},{28,24},{1,5},{5... | collective-permute-start | bytes 663560 | tf_op jit(solution)/shard_map/ppermute | solution.py:22
  198.5 16.8 %collective-permute-start.62 = (bf16[48,2304]{1,0:T(8,128)(2,1)S(1)}, bf16[48,2304]{1,0:T(8,128)(2,1)S(1)}, u32[]{:S(2)}, u32[]{:S(2)}) collective-permute-start(bf16[48,2304]{1,0:T(8,128)(2,1)S(1)} %collective-permute-done.57.refs_5_), channel_id=1, source_target_pairs={{0,4},{4,0},{8,12},{12,8},{16,20},{20,16},{24,28},{28,24},{1,5},{5... | collective-permute-start | bytes 663560 | tf_op jit(solution)/shard_map/ppermute | solution.py:22
  199.1 14.7 %collective-permute-start.44 = (bf16[48,1536]{1,0:T(8,128)(2,1)S(1)}, bf16[48,1536]{1,0:T(8,128)(2,1)S(1)}, u32[]{:S(2)}, u32[]{:S(2)}) collective-permute-start(bf16[48,1536]{1,0:T(8,128)(2,1)S(1)} %collective-permute-done.41.refs_1_), channel_id=1, source_target_pairs={{0,4},{4,0},{8,12},{12,8},{16,20},{20,16},{24,28},{28,24},{1,5},{5... | collective-permute-start | bytes 442376 | tf_op jit(solution)/shard_map/ppermute | solution.py:22
  200.5 14.8 %collective-permute-start.47 = (bf16[48,1536]{1,0:T(8,128)(2,1)S(1)}, bf16[48,1536]{1,0:T(8,128)(2,1)S(1)}, u32[]{:S(2)}, u32[]{:S(2)}) collective-permute-start(bf16[48,1536]{1,0:T(8,128)(2,1)S(1)} %collective-permute-done.42.refs_0_), channel_id=1, source_target_pairs={{0,4},{4,0},{8,12},{12,8},{16,20},{20,16},{24,28},{28,24},{1,5},{5... | collective-permute-start | bytes 442376 | tf_op jit(solution)/shard_map/ppermute | solution.py:22
  (107 other events, 1073.5 us)

commit v3 on v2

--- a/solution.py
+++ b/solution.py
@@ -340,10 +340,18 @@
     def body(index, *refs):
         ins = refs[:count]
         outs = refs[count + given : count + given + len(widths)]
-        wides, sem = refs[count + given + len(widths) : -1], refs[-1]
+        scratch = refs[count + given + len(widths) :]
+        held, wides, (fetched, sem) = scratch[:count], scratch[count:-2], scratch[-2:]
+        fetches = [
+            pltpu.make_async_copy(ref, block, fetched.at[i])
+            for i, (ref, block) in enumerate(zip(ins, held))
+        ]
+        for fetch in fetches:
+            fetch.start()
         copies = []
-        for ref, wide, (_, offset, spans) in zip(ins, wides, jobs):
+        for fetch, ref, wide, (_, offset, spans) in zip(fetches, held, wides, jobs):
             share = ref.shape[0]
+            fetch.wait()
             wide[...] = ref[...].astype(F32)
             start = pl.multiple_of((index[0] ^ offset) * share, share)
             for which, low, high, place in spans:
@@ -357,16 +365,16 @@
         for copy in copies:
             copy.wait()
 
-    space = pl.BlockSpec(memory_space=pltpu.MemorySpace.VMEM)
     whole = pl.BlockSpec(memory_space=pl.ANY)
     return pl.pallas_call(
         body,
         out_shape=[jax.ShapeDtypeStruct((total, width), F32) for width in widths],
         in_specs=[pl.BlockSpec(memory_space=pltpu.MemorySpace.SMEM)]
-        + [space] * count
-        + [whole] * given,
+        + [whole] * (count + given),
         out_specs=[whole] * len(widths),
-        scratch_shapes=[pltpu.VMEM(array.shape, F32) for array, _, _ in jobs]
+        scratch_shapes=[pltpu.VMEM(array.shape, BF16) for array, _, _ in jobs]
+        + [pltpu.VMEM(array.shape, F32) for array, _, _ in jobs]
+        + [pltpu.SemaphoreType.DMA((count,))]
         + [pltpu.SemaphoreType.DMA((sum(len(spans) for _, _, spans in jobs),))],
         input_output_aliases={count + 1 + j: j for j in range(given)},
         compiler_params=pltpu.CompilerParams(vmem_limit_bytes=56 * 1024 * 1024),

time: 221 us -> 220 us (level)
  no operation moved by 1% of the time
where the time goes in v3:
time: 220 us
  waiting for transfers between devices  77.1 us (35%)
  starting transfers between devices  76.6 us (35%)
  Pallas kernels  35.3 us (16%)
  local copies, waits for them, and re-layouts  13.7 us (6%)
  other arithmetic  10.2 us (5%)
  matrix products  5.07 us (2%)
    ppermute x72, waiting for transfers between devices, swap(): return lax.ppermute(value, axis, [(i, i ^ offset) for i in range(size)])  77.1 us
    ppermute x72, starting transfers between devices, swap(): return lax.ppermute(value, axis, [(i, i ^ offset) for i in range(size)])  76.6 us
    pallas_call x5, Pallas kernels, call(): pl.pallas_call(body, out_shape=[jax.ShapeDtypeStruct(shape, dtype) for sh...  29.3 us
    dynamic_slice x11, local copies, waits for them, and re-layouts, columns(): lax.dynamic_slice_in_dim(arr, owner * block + low, block, arr.ndim - 1)  7.59 us
    pallas_call x2, Pallas kernels, rows_in_place(): pl.pallas_call(body, out_shape=[jax.ShapeDtypeStruct((total, width), F32)...  6 us
  transfers between devices with their start and end apart: 72, of which 30 were waited for; matrix products, arithmetic and copies ran while one was open for 10% of the time, Pallas kernels for 9%

profile of v3, /device:TPU:0, one launch (start us, length us, event | category | flops | bytes accessed | tf_op | source)
XLA Modules:
  0.0 219.7 jit_solution(3090458559952245274)
XLA Ops:
  2.7 2.4 %collective-permute-start.5 = (bf16[1,128,384]{2,1,0:T(8,128)(2,1)}, bf16[1,128,384]{2,1,0:T(8,128)(2,1)}, u32[]{:S(2)}, u32[]{:S(2)}) collective-permute-start(bf16[1,128,384]{2,1,0:T(8,128)(2,1)} %get-tuple-element.93), channel_id=1, source_target_pairs={{0,3},{1,2},{2,1},{3,0},{4,7},{5,6},{6,5},{7,4},{8,11},{9,10},{10,... | collective-permute-start | bytes 294920 | tf_op jit(solution)/shard_map/ppermute | solution.py:22
  23.5 8.4 %collective-permute-done.4.refs_6_ = bf16[1,128,384]{2,1,0:T(8,128)(2,1)S(1)} collective-permute-done((bf16[1,128,384]{2,1,0:T(8,128)(2,1)S(1)}, bf16[1,128,384]{2,1,0:T(8,128)(2,1)S(1)}, u32[]{:S(2)}, u32[]{:S(2)}) %collective-permute-start.4) | collective-permute-done | bytes 98336 | tf_op jit(solution)/shard_map/ppermute | solution.py:22
  34.2 5.1 %shard_map.121 = (bf16[512,384]{1,0:T(8,128)(2,1)}, f32[2,512]{1,0:T(2,128)}) custom-call(s32[1]{0:T(128)} %bitcast.1.index, bf16[3,128,384]{2,1,0:T(8,128)(2,1)} %pad_maximum_fusion.4.refs_0_, bf16[3,128,384]{2,1,0:T(8,128)(2,1)} %collective-permute-done.refs_1_, bf16[3,128,384]{2,1,0:T(8,128)(2,1)} %collective-permute-done.1.refs_2_, ...), custom_call_target="tpu_custom_call" | custom-call | tf_op jit(solution)/shard_map/pallas_call | solution.py:60
  41.1 2.7 %collective-permute-start.17 = (bf16[2,48,768]{2,1,0:T(8,128)(2,1)S(1)}, bf16[2,48,768]{2,1,0:T(8,128)(2,1)}, u32[]{:S(2)}, u32[]{:S(2)}) collective-permute-start(bf16[2,48,768]{2,1,0:T(8,128)(2,1)S(1)} %pad_maximum_fusion.9.refs_6_), channel_id=1, source_target_pairs={{0,16},{4,20},{8,24},{12,28},{16,0},{20,4},{24,8},{28,12},{1,17},{... | collective-permute-start | bytes 442376 | tf_op jit(solution)/shard_map/ppermute | solution.py:22
  48.3 2.8 %collective-permute-done.17.refs_10_ = bf16[2,48,768]{2,1,0:T(8,128)(2,1)} collective-permute-done((bf16[2,48,768]{2,1,0:T(8,128)(2,1)S(1)}, bf16[2,48,768]{2,1,0:T(8,128)(2,1)}, u32[]{:S(2)}, u32[]{:S(2)}) %collective-permute-start.17) | collective-permute-done | bytes 147488 | tf_op jit(solution)/shard_map/ppermute | solution.py:22
  65.5 3.2 %collective-permute-done.16.refs_9_ = bf16[2,48,768]{2,1,0:T(8,128)(2,1)S(1)} collective-permute-done((bf16[2,48,768]{2,1,0:T(8,128)(2,1)S(1)}, bf16[2,48,768]{2,1,0:T(8,128)(2,1)S(1)}, u32[]{:S(2)}, u32[]{:S(2)}) %collective-permute-start.16) | collective-permute-done | bytes 147488 | tf_op jit(solution)/shard_map/ppermute | solution.py:22
  71.5 8.1 %shard_map.122 = (bf16[512,1536]{1,0:T(8,128)(2,1)}, f32[512,768]{1,0:T(8,128)}, bf16[512,384]{1,0:T(8,128)(2,1)}, f32[512,384]{1,0:T(8,128)}, f32[2,512]{1,0:T(2,128)}) custom-call(s32[1]{0:T(128)} %bitcast.index, bf16[512,384]{1,0:T(8,128)(2,1)} %get-tuple-element.40.refs_0_, bf16[512,384]{1,0:T(8,128)(2,1)} %copy-done.11, ...), custom_call_target="tpu_custom_call" | custom-call | tf_op jit(solution)/shard_map/pallas_call | solution.py:60
  85.1 4.0 %shard_map.123 = (bf16[384,512]{1,0:T(8,128)(2,1)}, f32[512,384]{1,0:T(8,128)}, f32[512,384]{1,0:T(8,128)}, f32[1,512]{1,0:T(1,128)}, f32[2,512]{1,0:T(2,128)}) custom-call(f32[512,384]{1,0:T(8,128)} %get-tuple-element.44.z_ref, f32[1,384]{1,0:T(1,128)} %dynamic_slice.227.gain_ref, f32[512,384]{1,0:T(8,128)} %fusion.22.ds_ref, ...), custom_call_target="tpu_custom_call" | custom-call | tf_op jit(solution)/shard_map/pallas_call | solution.py:60
  98.2 5.9 %shard_map.124 = (bf16[512,768]{1,0:T(8,128)(2,1)}, bf16[512,384]{1,0:T(8,128)(2,1)}) custom-call(f32[512,384]{1,0:T(8,128)} %get-tuple-element.48.e_ref, f32[512,384]{1,0:T(8,128)} %get-tuple-element.49.zhat_ref, f32[1,512]{1,0:T(1,128)} %get-tuple-element.50.inv_ref, f32[512,768]{1,0:T(8,128)} %get-tuple-element.51.p_ref, ...), custom_call_target="tpu_custom_call" | custom-call | tf_op jit(solution)/shard_map/pallas_call | solution.py:60
  106.1 3.0 %collective-permute-start.34 = (bf16[2,48,768]{2,1,0:T(8,128)(2,1)S(1)}, bf16[2,48,768]{2,1,0:T(8,128)(2,1)}, u32[]{:S(2)}, u32[]{:S(2)}) collective-permute-start(bf16[2,48,768]{2,1,0:T(8,128)(2,1)S(1)} %fusion.9), channel_id=1, source_target_pairs={{0,16},{4,20},{8,24},{12,28},{16,0},{20,4},{24,8},{28,12},{1,17},{... | collective-permute-start | bytes 442376 | tf_op jit(solution)/shard_map/ppermute | solution.py:22
  113.3 6.2 %shard_map.125 = f32[32,384]{1,0:T(8,128)} custom-call(bf16[512,384]{1,0:T(8,128)(2,1)} %get-tuple-element.58.dz_ref, bf16[512,384]{1,0:T(8,128)(2,1)} %get-tuple-element.59.y_ref), custom_call_target="tpu_custom_call" | custom-call | tf_op jit(solution)/shard_map/pallas_call | solution.py:60
  120.5 5.2 %collective-permute-done.32 = bf16[2,2,4,48,384]{4,3,2,1,0:T(8,128)(2,1)} collective-permute-done((bf16[2,2,4,48,384]{4,3,2,1,0:T(8,128)(2,1)S(1)}, bf16[2,2,4,48,384]{4,3,2,1,0:T(8,128)(2,1)}, u32[]{:S(2)}, u32[]{:S(2)}) %collective-permute-start.32) | collective-permute-done | bytes 589856 | tf_op jit(solution)/shard_map/ppermute | solution.py:22
  130.7 2.7 %collective-permute-start.50 = (bf16[2,4,48,384]{3,2,1,0:T(8,128)(2,1)S(1)}, bf16[2,4,48,384]{3,2,1,0:T(8,128)(2,1)S(1)}, u32[]{:S(2)}, u32[]{:S(2)}) collective-permute-start(bf16[2,4,48,384]{3,2,1,0:T(8,128)(2,1)S(1)} %fusion.3), channel_id=1, source_target_pairs={{0,16},{4,20},{8,24},{12,28},{16,0},{20,4},{24,8},{28,12},{1,17},{... | collective-permute-start | bytes 884744 | tf_op jit(solution)/shard_map/ppermute | solution.py:22
  134.6 7.9 %collective-permute-done.35 = bf16[2,4,48,384]{3,2,1,0:T(8,128)(2,1)S(1)} collective-permute-done((bf16[2,4,48,384]{3,2,1,0:T(8,128)(2,1)S(1)}, bf16[2,4,48,384]{3,2,1,0:T(8,128)(2,1)S(1)}, u32[]{:S(2)}, u32[]{:S(2)}) %collective-permute-start.35) | collective-permute-done | bytes 294944 | tf_op jit(solution)/shard_map/ppermute | solution.py:22
  142.7 2.9 %collective-permute-start.37 = (bf16[4,48,384]{2,1,0:T(8,128)(2,1)S(1)}, bf16[4,48,384]{2,1,0:T(8,128)(2,1)S(1)}, u32[]{:S(2)}, u32[]{:S(2)}) collective-permute-start(bf16[4,48,384]{2,1,0:T(8,128)(2,1)S(1)} %fusion.10), channel_id=1, source_target_pairs={{0,16},{4,20},{8,24},{12,28},{16,0},{20,4},{24,8},{28,12},{1,17},{... | collective-permute-start | bytes 442376 | tf_op jit(solution)/shard_map/ppermute | solution.py:22
  145.6 2.6 %collective-permute-done.50 = bf16[2,4,48,384]{3,2,1,0:T(8,128)(2,1)S(1)} collective-permute-done((bf16[2,4,48,384]{3,2,1,0:T(8,128)(2,1)S(1)}, bf16[2,4,48,384]{3,2,1,0:T(8,128)(2,1)S(1)}, u32[]{:S(2)}, u32[]{:S(2)}) %collective-permute-start.50) | collective-permute-done | bytes 294944 | tf_op jit(solution)/shard_map/ppermute | solution.py:22
  148.8 3.2 %collective-permute-done.37 = bf16[4,48,384]{2,1,0:T(8,128)(2,1)S(1)} collective-permute-done((bf16[4,48,384]{2,1,0:T(8,128)(2,1)S(1)}, bf16[4,48,384]{2,1,0:T(8,128)(2,1)S(1)}, u32[]{:S(2)}, u32[]{:S(2)}) %collective-permute-start.37) | collective-permute-done | bytes 147488 | tf_op jit(solution)/shard_map/ppermute | solution.py:22
  167.1 2.5 %collective-permute-start.68 = (bf16[48,768]{1,0:T(8,128)(2,1)S(1)}, bf16[48,768]{1,0:T(8,128)(2,1)S(1)}, u32[]{:S(2)}, u32[]{:S(2)}) collective-permute-start(bf16[48,768]{1,0:T(8,128)(2,1)S(1)} %collective-permute-done.65.refs_7_), channel_id=1, source_target_pairs={{0,8},{4,12},{8,0},{12,4},{16,24},{20,28},{24,16},{28,20},{1,9},{5... | collective-permute-start | bytes 221192 | tf_op jit(solution)/shard_map/ppermute | solution.py:22
  169.5 5.9 %collective-permute-done.64.refs_10_ = bf16[48,768]{1,0:T(8,128)(2,1)S(1)} collective-permute-done((bf16[48,768]{1,0:T(8,128)(2,1)S(1)}, bf16[48,768]{1,0:T(8,128)(2,1)S(1)}, u32[]{:S(2)}, u32[]{:S(2)}) %collective-permute-start.64) | collective-permute-done | bytes 73760 | tf_op jit(solution)/shard_map/ppermute | solution.py:22
  184.3 3.4 %collective-permute-start.58 = (bf16[48,2304]{1,0:T(8,128)(2,1)S(1)}, bf16[48,2304]{1,0:T(8,128)(2,1)S(1)}, u32[]{:S(2)}, u32[]{:S(2)}) collective-permute-start(bf16[48,2304]{1,0:T(8,128)(2,1)S(1)} %pad_maximum_fusion.8.refs_3_), channel_id=1, source_target_pairs={{0,4},{4,0},{8,12},{12,8},{16,20},{20,16},{24,28},{28,24},{1,5},{5... | collective-permute-start | bytes 663560 | tf_op jit(solution)/shard_map/ppermute | solution.py:22
  190.3 3.5 %collective-permute-done.60.refs_5_ = bf16[48,2304]{1,0:T(8,128)(2,1)S(1)} collective-permute-done((bf16[48,2304]{1,0:T(8,128)(2,1)S(1)}, bf16[48,2304]{1,0:T(8,128)(2,1)S(1)}, u32[]{:S(2)}, u32[]{:S(2)}) %collective-permute-start.60) | collective-permute-done | bytes 221216 | tf_op jit(solution)/shard_map/ppermute | solution.py:22
  201.8 2.5 %shard_map.126 = (f32[384,3072]{1,0:T(8,128)}, f32[384,1536]{1,0:T(8,128)}) custom-call(s32[1]{0:T(128)} %bitcast.index, bf16[48,1536]{1,0:T(8,128)(2,1)} %copy-done.5, bf16[48,1536]{1,0:T(8,128)(2,1)} %copy-done.27, bf16[48,1536]{1,0:T(8,128)(2,1)} %copy-done.24, bf16[48,2304]{1,0:T(8,128)(2,1)} %copy-done.3, bf16[48,2304]{1,0:T(8,128)(2,1)} %copy-done.16, ...), custom_call_target="tpu_custom_call" | custom-call | tf_op jit(solution)/shard_map/pallas_call | solution.py:369
  204.3 9.4 %collective-permute-done.44.refs_2_ = bf16[48,1536]{1,0:T(8,128)(2,1)S(1)} collective-permute-done((bf16[48,1536]{1,0:T(8,128)(2,1)S(1)}, bf16[48,1536]{1,0:T(8,128)(2,1)S(1)}, u32[]{:S(2)}, u32[]{:S(2)}) %collective-permute-start.44) | collective-permute-done | bytes 147488 | tf_op jit(solution)/shard_map/ppermute | solution.py:22
  216.1 3.5 %shard_map.127 = (f32[384,3072]{1,0:T(8,128)}, f32[384,1536]{1,0:T(8,128)}) custom-call(s32[1]{0:T(128)} %bitcast.index, bf16[48,1536]{1,0:T(8,128)(2,1)} %copy-done.34, bf16[48,1536]{1,0:T(8,128)(2,1)} %copy-done.32, bf16[48,1536]{1,0:T(8,128)(2,1)} %copy-done.35, bf16[48,1536]{1,0:T(8,128)(2,1)} %copy-done.33, ...), custom_call_target="tpu_custom_call", output_to_operand_aliasing={{0}: (17, {}), {1}: (18, {})} | custom-call | tf_op jit(solution)/shard_map/pallas_call | solution.py:369
  (314 shorter events, 111.3 us)
Async XLA Ops:
  2.7 14.9 %collective-permute-start.5 = (bf16[1,128,384]{2,1,0:T(8,128)(2,1)}, bf16[1,128,384]{2,1,0:T(8,128)(2,1)}, u32[]{:S(2)}, u32[]{:S(2)}) collective-permute-start(bf16[1,128,384]{2,1,0:T(8,128)(2,1)} %get-tuple-element.93), channel_id=1, source_target_pairs={{0,3},{1,2},{2,1},{3,0},{4,7},{5,6},{6,5},{7,4},{8,11},{9,10},{10,... | collective-permute-start | bytes 294920 | tf_op jit(solution)/shard_map/ppermute | solution.py:22
  7.6 26.2 %collective-permute-start.1 = (bf16[3,128,384]{2,1,0:T(8,128)(2,1)}, bf16[3,128,384]{2,1,0:T(8,128)(2,1)}, u32[]{:S(2)}, u32[]{:S(2)}) collective-permute-start(bf16[3,128,384]{2,1,0:T(8,128)(2,1)} %pad_maximum_fusion.6), channel_id=1, source_target_pairs={{0,2},{1,3},{2,0},{3,1},{4,6},{5,7},{6,4},{7,5},{8,10},{9,11},{10,... | collective-permute-start | bytes 884744 | tf_op jit(solution)/shard_map/ppermute | solution.py:22
  9.8 24.4 %collective-permute-start = (bf16[3,128,384]{2,1,0:T(8,128)(2,1)}, bf16[3,128,384]{2,1,0:T(8,128)(2,1)}, u32[]{:S(2)}, u32[]{:S(2)}) collective-permute-start(bf16[3,128,384]{2,1,0:T(8,128)(2,1)} %pad_maximum_fusion.5), channel_id=1, source_target_pairs={{0,1},{1,0},{2,3},{3,2},{4,5},{5,4},{6,7},{7,6},{8,9},{9,8},{10,11... | collective-permute-start | bytes 884744 | tf_op jit(solution)/shard_map/ppermute | solution.py:22
  10.7 23.5 %collective-permute-start.2 = (bf16[3,128,384]{2,1,0:T(8,128)(2,1)}, bf16[3,128,384]{2,1,0:T(8,128)(2,1)}, u32[]{:S(2)}, u32[]{:S(2)}) collective-permute-start(bf16[3,128,384]{2,1,0:T(8,128)(2,1)} %pad_maximum_fusion.7), channel_id=1, source_target_pairs={{0,3},{1,2},{2,1},{3,0},{4,7},{5,6},{6,5},{7,4},{8,11},{9,10},{10,... | collective-permute-start | bytes 884744 | tf_op jit(solution)/shard_map/ppermute | solution.py:22
  17.5 34.1 %collective-permute-start.9 = (bf16[2,1,128,1536]{3,2,1,0:T(8,128)(2,1)S(1)}, bf16[2,1,128,1536]{3,2,1,0:T(8,128)(2,1)}, u32[]{:S(2)}, u32[]{:S(2)}) collective-permute-start(bf16[2,1,128,1536]{3,2,1,0:T(8,128)(2,1)S(1)} %pad_maximum_fusion.1), channel_id=1, source_target_pairs={{0,1},{1,0},{2,3},{3,2},{4,5},{5,4},{6,7},{7,6},{8,9},{9,8},{10,11... | collective-permute-start | bytes 2359304 | tf_op jit(solution)/shard_map/ppermute | solution.py:22
  53.3 17.1 %collective-permute-start.11 = (bf16[384,768]{1,0:T(8,128)(2,1)S(1)}, bf16[384,768]{1,0:T(8,128)(2,1)S(1)}, u32[]{:S(2)}, u32[]{:S(2)}) collective-permute-start(bf16[384,768]{1,0:T(8,128)(2,1)S(1)} %copy-done.7), channel_id=1, source_target_pairs={{0,1},{1,0},{2,3},{3,2},{4,5},{5,4},{6,7},{7,6},{8,9},{9,8},{10,11... | collective-permute-start | bytes 1769480 | tf_op jit(solution)/shard_map/ppermute | solution.py:22
  54.9 15.6 %collective-permute-start.6 = (bf16[512,384]{1,0:T(8,128)(2,1)S(1)}, bf16[512,384]{1,0:T(8,128)(2,1)S(1)}, u32[]{:S(2)}, u32[]{:S(2)}) collective-permute-start(bf16[512,384]{1,0:T(8,128)(2,1)S(1)} %copy-done.9), channel_id=1, source_target_pairs={{0,1},{1,0},{2,3},{3,2},{4,5},{5,4},{6,7},{7,6},{8,9},{9,8},{10,11... | collective-permute-start | bytes 1179656 | tf_op jit(solution)/shard_map/ppermute | solution.py:22
  91.2 12.8 %collective-permute-start.27 = (bf16[2,2,48,768]{3,2,0,1:T(8,128)(2,1)S(1)}, bf16[2,2,48,768]{3,2,0,1:T(8,128)(2,1)S(1)}, u32[]{:S(2)}, u32[]{:S(2)}) collective-permute-start(bf16[2,2,48,768]{3,2,0,1:T(8,128)(2,1)S(1)} %fusion.4), channel_id=1, source_target_pairs={{0,4},{4,0},{8,12},{12,8},{16,20},{20,16},{24,28},{28,24},{1,5},{5... | collective-permute-start | bytes 884744 | tf_op jit(solution)/shard_map/ppermute | solution.py:22
  104.9 14.6 %collective-permute-start.33 = (bf16[2,48,768]{2,1,0:T(8,128)(2,1)}, bf16[2,48,768]{2,1,0:T(8,128)(2,1)S(1)}, u32[]{:S(2)}, u32[]{:S(2)}) collective-permute-start(bf16[2,48,768]{2,1,0:T(8,128)(2,1)} %fusion.8), channel_id=1, source_target_pairs={{0,8},{4,12},{8,0},{12,4},{16,24},{20,28},{24,16},{28,20},{1,9},{5... | collective-permute-start | bytes 442376 | tf_op jit(solution)/shard_map/ppermute | solution.py:22
  106.1 13.4 %collective-permute-start.34 = (bf16[2,48,768]{2,1,0:T(8,128)(2,1)S(1)}, bf16[2,48,768]{2,1,0:T(8,128)(2,1)}, u32[]{:S(2)}, u32[]{:S(2)}) collective-permute-start(bf16[2,48,768]{2,1,0:T(8,128)(2,1)S(1)} %fusion.9), channel_id=1, source_target_pairs={{0,16},{4,20},{8,24},{12,28},{16,0},{20,4},{24,8},{28,12},{1,17},{... | collective-permute-start | bytes 442376 | tf_op jit(solution)/shard_map/ppermute | solution.py:22
  111.6 14.2 %collective-permute-start.32 = (bf16[2,2,4,48,384]{4,3,2,1,0:T(8,128)(2,1)S(1)}, bf16[2,2,4,48,384]{4,3,2,1,0:T(8,128)(2,1)}, u32[]{:S(2)}, u32[]{:S(2)}) collective-permute-start(bf16[2,2,4,48,384]{4,3,2,1,0:T(8,128)(2,1)S(1)} %fusion), channel_id=1, source_target_pairs={{0,4},{4,0},{8,12},{12,8},{16,20},{20,16},{24,28},{28,24},{1,5},{5... | collective-permute-start | bytes 1769480 | tf_op jit(solution)/shard_map/ppermute | solution.py:22
  112.2 18.3 %collective-permute-start.49 = (bf16[2,2,4,48,384]{4,3,2,1,0:T(8,128)(2,1)S(1)}, bf16[2,2,4,48,384]{4,3,2,1,0:T(8,128)(2,1)S(1)}, u32[]{:S(2)}, u32[]{:S(2)}) collective-permute-start(bf16[2,2,4,48,384]{4,3,2,1,0:T(8,128)(2,1)S(1)} %fusion.1), channel_id=1, source_target_pairs={{0,8},{4,12},{8,0},{12,4},{16,24},{20,28},{24,16},{28,20},{1,9},{5... | collective-permute-start | bytes 1769480 | tf_op jit(solution)/shard_map/ppermute | solution.py:22
  129.5 13.0 %collective-permute-start.35 = (bf16[2,4,48,384]{3,2,1,0:T(8,128)(2,1)S(1)}, bf16[2,4,48,384]{3,2,1,0:T(8,128)(2,1)S(1)}, u32[]{:S(2)}, u32[]{:S(2)}) collective-permute-start(bf16[2,4,48,384]{3,2,1,0:T(8,128)(2,1)S(1)} %fusion.2), channel_id=1, source_target_pairs={{0,8},{4,12},{8,0},{12,4},{16,24},{20,28},{24,16},{28,20},{1,9},{5... | collective-permute-start | bytes 884744 | tf_op jit(solution)/shard_map/ppermute | solution.py:22
  130.7 17.5 %collective-permute-start.50 = (bf16[2,4,48,384]{3,2,1,0:T(8,128)(2,1)S(1)}, bf16[2,4,48,384]{3,2,1,0:T(8,128)(2,1)S(1)}, u32[]{:S(2)}, u32[]{:S(2)}) collective-permute-start(bf16[2,4,48,384]{3,2,1,0:T(8,128)(2,1)S(1)} %fusion.3), channel_id=1, source_target_pairs={{0,16},{4,20},{8,24},{12,28},{16,0},{20,4},{24,8},{28,12},{1,17},{... | collective-permute-start | bytes 884744 | tf_op jit(solution)/shard_map/ppermute | solution.py:22
  133.4 29.1 %collective-permute-start.65 = (bf16[48,768]{1,0:T(8,128)(2,1)S(1)}, bf16[48,768]{1,0:T(8,128)(2,1)S(1)}, u32[]{:S(2)}, u32[]{:S(2)}) collective-permute-start(bf16[48,768]{1,0:T(8,128)(2,1)S(1)} %fusion.12.refs_6_), channel_id=1, source_target_pairs={{0,4},{4,0},{8,12},{12,8},{16,20},{20,16},{24,28},{28,24},{1,5},{5... | collective-permute-start | bytes 221192 | tf_op jit(solution)/shard_map/ppermute | solution.py:22
  159.5 28.1 %collective-permute-start.56 = (bf16[48,2304]{1,0:T(8,128)(2,1)S(1)}, bf16[48,2304]{1,0:T(8,128)(2,1)S(1)}, u32[]{:S(2)}, u32[]{:S(2)}) collective-permute-start(bf16[48,2304]{1,0:T(8,128)(2,1)S(1)} %pad_maximum_fusion.8.refs_3_), channel_id=1, source_target_pairs={{0,16},{4,20},{8,24},{12,28},{16,0},{20,4},{24,8},{28,12},{1,17},{... | collective-permute-start | bytes 663560 | tf_op jit(solution)/shard_map/ppermute | solution.py:22
  161.7 13.7 %collective-permute-start.64 = (bf16[48,768]{1,0:T(8,128)(2,1)S(1)}, bf16[48,768]{1,0:T(8,128)(2,1)S(1)}, u32[]{:S(2)}, u32[]{:S(2)}) collective-permute-start(bf16[48,768]{1,0:T(8,128)(2,1)S(1)} %fusion.12.refs_6_), channel_id=1, source_target_pairs={{0,16},{4,20},{8,24},{12,28},{16,0},{20,4},{24,8},{28,12},{1,17},{... | collective-permute-start | bytes 221192 | tf_op jit(solution)/shard_map/ppermute | solution.py:22
  162.5 14.3 %collective-permute-start.66 = (bf16[48,768]{1,0:T(8,128)(2,1)S(1)}, bf16[48,768]{1,0:T(8,128)(2,1)S(1)}, u32[]{:S(2)}, u32[]{:S(2)}) collective-permute-start(bf16[48,768]{1,0:T(8,128)(2,1)S(1)} %collective-permute-done.65.refs_7_), channel_id=1, source_target_pairs={{0,16},{4,20},{8,24},{12,28},{16,0},{20,4},{24,8},{28,12},{1,17},{... | collective-permute-start | bytes 221192 | tf_op jit(solution)/shard_map/ppermute | solution.py:22
  164.6 19.6 %collective-permute-start.45 = (bf16[48,1536]{1,0:T(8,128)(2,1)S(1)}, bf16[48,1536]{1,0:T(8,128)(2,1)S(1)}, u32[]{:S(2)}, u32[]{:S(2)}) collective-permute-start(bf16[48,1536]{1,0:T(8,128)(2,1)S(1)} %pad_maximum_fusion.11.refs_0_), channel_id=1, source_target_pairs={{0,8},{4,12},{8,0},{12,4},{16,24},{20,28},{24,16},{28,20},{1,9},{5... | collective-permute-start | bytes 442376 | tf_op jit(solution)/shard_map/ppermute | solution.py:22
  193.8 20.0 %collective-permute-start.61 = (bf16[48,2304]{1,0:T(8,128)(2,1)S(1)}, bf16[48,2304]{1,0:T(8,128)(2,1)S(1)}, u32[]{:S(2)}, u32[]{:S(2)}) collective-permute-start(bf16[48,2304]{1,0:T(8,128)(2,1)S(1)} %collective-permute-done.60.refs_5_), channel_id=1, source_target_pairs={{0,4},{4,0},{8,12},{12,8},{16,20},{20,16},{24,28},{28,24},{1,5},{5... | collective-permute-start | bytes 663560 | tf_op jit(solution)/shard_map/ppermute | solution.py:22
  196.2 17.6 %collective-permute-start.59 = (bf16[48,2304]{1,0:T(8,128)(2,1)S(1)}, bf16[48,2304]{1,0:T(8,128)(2,1)S(1)}, u32[]{:S(2)}, u32[]{:S(2)}) collective-permute-start(bf16[48,2304]{1,0:T(8,128)(2,1)S(1)} %collective-permute-done.56.refs_4_), channel_id=1, source_target_pairs={{0,4},{4,0},{8,12},{12,8},{16,20},{20,16},{24,28},{28,24},{1,5},{5... | collective-permute-start | bytes 663560 | tf_op jit(solution)/shard_map/ppermute | solution.py:22
  198.5 16.8 %collective-permute-start.62 = (bf16[48,2304]{1,0:T(8,128)(2,1)S(1)}, bf16[48,2304]{1,0:T(8,128)(2,1)S(1)}, u32[]{:S(2)}, u32[]{:S(2)}) collective-permute-start(bf16[48,2304]{1,0:T(8,128)(2,1)S(1)} %collective-permute-done.57.refs_5_), channel_id=1, source_target_pairs={{0,4},{4,0},{8,12},{12,8},{16,20},{20,16},{24,28},{28,24},{1,5},{5... | collective-permute-start | bytes 663560 | tf_op jit(solution)/shard_map/ppermute | solution.py:22
  199.1 14.7 %collective-permute-start.44 = (bf16[48,1536]{1,0:T(8,128)(2,1)S(1)}, bf16[48,1536]{1,0:T(8,128)(2,1)S(1)}, u32[]{:S(2)}, u32[]{:S(2)}) collective-permute-start(bf16[48,1536]{1,0:T(8,128)(2,1)S(1)} %collective-permute-done.41.refs_1_), channel_id=1, source_target_pairs={{0,4},{4,0},{8,12},{12,8},{16,20},{20,16},{24,28},{28,24},{1,5},{5... | collective-permute-start | bytes 442376 | tf_op jit(solution)/shard_map/ppermute | solution.py:22
  200.5 14.8 %collective-permute-start.47 = (bf16[48,1536]{1,0:T(8,128)(2,1)S(1)}, bf16[48,1536]{1,0:T(8,128)(2,1)S(1)}, u32[]{:S(2)}, u32[]{:S(2)}) collective-permute-start(bf16[48,1536]{1,0:T(8,128)(2,1)S(1)} %collective-permute-done.42.refs_0_), channel_id=1, source_target_pairs={{0,4},{4,0},{8,12},{12,8},{16,20},{20,16},{24,28},{28,24},{1,5},{5... | collective-permute-start | bytes 442376 | tf_op jit(solution)/shard_map/ppermute | solution.py:22
  (107 other events, 1072.9 us)
